TPU v7x, 256 devices: a whole 4x4x8 slice. The times are simulated.
256 devices in a mesh: samp: 32 (over z_hi, y, x), feat: 8 (over z_lo, core).
Axes of the slice: x: 4, y: 4, z: 8 (z_hi: 2, z_lo: 4; z = z_hi * 4 + z_lo), core: 2. Of those that a mesh axis runs over, the one named last changes fastest.
Arguments:
- counters: bfloat16 [32768, 512], P('samp'), may hold values from -6 to 6
- frequencies: bfloat16 [512, 4096], P(None, 'feat'), may hold values from -0.25 to 0.25
- phases: bfloat16 [1, 4096], P(None, 'feat'), may hold values from -3.140625 to 3.140625
- targets: bfloat16 [32768, 64], P('samp'), may hold values from -6 to 6
Outputs:
- solution: float32 [4096, 64], P('samp')
- residual: float32 [4096, 64], P('samp')
- gram: float32 [4096, 4096], P('samp', 'feat')
All inputs are finite; a program needn't handle non-finite values.
Results may differ from a plain program's by a relative error of at most 0.0035.
Values may be sent and summed in bfloat16 or wider, within the bound.
A program may use at most 64 MiB of HBM per device.

v0:
```python
import math

import jax
import jax.numpy as jnp
from jax import lax
from jax.sharding import PartitionSpec as P

ITERS = 2


RIDGE = 0.05


def on_device(counters, frequencies, phases, targets):
    rows = counters.shape[0]
    block_width = frequencies.shape[1]
    mixed = jnp.dot(counters, frequencies, preferred_element_type=jnp.float32)
    local_feats = jnp.cos(mixed + phases.astype(jnp.float32)).astype(jnp.bfloat16)
    features_all = lax.all_gather(local_feats, "feat", axis=1, tiled=True)
    joined = jnp.concatenate([local_feats, targets], axis=1)
    inner = (((0,), (0,)), ((), ()))
    reduced = lax.psum_scatter(
        lax.dot_general(features_all, joined, inner, preferred_element_type=jnp.float32),
        "samp",
        scatter_dimension=0,
        tiled=True,
    )
    samples = rows * lax.axis_size("samp")
    gram_block = reduced[:, :block_width] / samples
    right_side = reduced[:, block_width:] / math.sqrt(samples)
    feat_offset = lax.axis_index("feat") * block_width

    def squares(vector):
        return lax.psum(jnp.sum(vector * vector, axis=0), "samp")

    solution = jnp.zeros_like(right_side)
    residual = right_side
    direction = right_side
    norm_now = squares(residual)
    for iteration in range(ITERS):
        gathered = lax.all_gather(direction, "samp", axis=0, tiled=True)
        selected = lax.dynamic_slice_in_dim(gathered, feat_offset, block_width, 0)
        partial_value = jnp.dot(gram_block, selected, precision=lax.Precision.HIGHEST)
        image = lax.psum(partial_value, "feat") + RIDGE * direction
        curve = lax.psum(jnp.sum(direction * image, axis=0), "samp")
        step_size = norm_now / curve
        solution = solution + step_size * direction
        residual = residual - step_size * image
        norm_next = squares(residual)
        direction = residual + norm_next / norm_now * direction
        norm_now = norm_next
    return (solution, residual, gram_block)


def solution(mesh):
    return jax.shard_map(
        on_device,
        mesh=mesh,
        in_specs=(P("samp", None), P(None, "feat"), P(None, "feat"), P("samp", None)),
        out_specs=(P("samp", None), P("samp", None), P("samp", "feat")),
        check_vma=False,
    )
```

profile of v0, /device:TPU:1, one launch (start us, length us, event | category | flops | bytes accessed | tf_op | source)
XLA Modules:
  0.0 958.3 jit_solution(9429398603258121843)
XLA Ops:
  7.2 0.8 add.52
  8.0 0.4 copy-done
  8.4 9.2 cosine_convert_fusion
  17.7 95.6 %all-gather.4.cloned.1.call-done = bf16[1024,4096]{0,1:T(8,128)(2,1)} async-done(((bf16[1024,512]{0,1:T(8,128)(2,1)}), bf16[1024,4096]{0,1:T(8,128)(2,1)}) %all-gather.4.cloned.1.call-update) | async-done | bytes 8388624 | tf_op jit(solution)/shard_map/all_gather | solution.py:19
  113.3 9.9 %fusion = f32[4096,576]{0,1:T(8,128)} fusion(bf16[1024,4096]{0,1:T(8,128)(2,1)} %all-gather.4.cloned.1.call-done, bf16[1024,64]{0,1:T(8,128)(2,1)S(1)} %copy-done.1, bf16[1024,512]{0,1:T(8,128)(2,1)} %cosine_convert_fusion), kind=kOutput, calls=%fused_computation.1 | convolution fusion | flops 4834197504 | bytes 19005440 | tf_op jit(solution)/shard_map/dot_general | solution.py:23
  123.2 0.0 all-gather.6.cloned.1.call-start
  123.3 288.4 %reduce-scatter.2.cloned.1.call-done = f32[128,576]{0,1:T(8,128)} async-done(((f32[4096,576]{0,1:T(8,128)}), f32[128,576]{0,1:T(8,128)}) %reduce-scatter.2.cloned.1.call-update) | async-done | bytes 294928 | tf_op jit(solution)/shard_map/reduce_scatter | solution.py:22
  411.7 1.4 slice_multiply_fusion.1
  413.1 82.0 %all-gather.6.cloned.1.call-done = f32[4096,64]{0,1:T(8,128)} async-done(((f32[128,64]{0,1:T(8,128)}), f32[4096,64]{0,1:T(8,128)}) %all-gather.6.cloned.1.call-update) | async-done | bytes 1048592 | tf_op jit(solution)/shard_map/all_gather | solution.py:41
  495.2 1.3 fusion.6
  496.5 24.2 %psum.43 = f32[128,64]{0,1:T(8,128)S(1)} all-reduce(f32[128,64]{0,1:T(8,128)S(1)} %fusion.6), channel_id=1, replica_groups=mesh['samp'=32,'feat'=8] {'feat'}, use_global_device_ids=true, to_apply=%region_3.0 | all-reduce | flops 8192 | bytes 65536 | tf_op jit(solution)/shard_map/psum | solution.py:44
  520.6 0.9 multiply_reduce_fusion.2
  521.5 96.9 %all-reduce = (f32[64]{0:T(128)S(1)}, f32[64]{0:T(128)S(1)}) all-reduce(f32[64]{0:T(128)S(1)} %get-tuple-element.7, f32[64]{0:T(128)S(1)} %get-tuple-element.6), channel_id=1, replica_groups=mesh['samp'=32,'feat'=8] {'samp'}, use_global_device_ids=true, to_apply=%region_2.0 | all-reduce | flops 128 | bytes 1024 | tf_op jit(solution)/shard_map/psum | solution.py:34
  618.4 0.9 multiply_reduce_fusion.1
  619.4 94.6 %psum.45 = f32[64]{0:T(128)S(1)} all-reduce(f32[64]{0:T(128)S(1)} %get-tuple-element.12), channel_id=1, replica_groups=mesh['samp'=32,'feat'=8] {'samp'}, use_global_device_ids=true, to_apply=%region_7.0 | all-reduce | flops 64 | bytes 512 | tf_op jit(solution)/shard_map/psum | solution.py:34
  714.0 1.5 multiply_add_fusion.2
  715.5 1.0 slice_multiply_fusion
  716.4 0.8 copy.7
  717.3 109.8 %all-gather.8.cloned.1.call-done = f32[4096,64]{0,1:T(8,128)} async-done(((f32[128,64]{0,1:T(8,128)}), f32[4096,64]{0,1:T(8,128)}) %all-gather.8.cloned.1.call-update) | async-done | bytes 1048592 | tf_op jit(solution)/shard_map/all_gather | solution.py:41
  827.1 1.3 fusion.4
  828.4 24.2 %psum.46 = f32[128,64]{0,1:T(8,128)S(1)} all-reduce(f32[128,64]{0,1:T(8,128)S(1)} %fusion.4), channel_id=1, replica_groups=mesh['samp'=32,'feat'=8] {'feat'}, use_global_device_ids=true, to_apply=%region_8.0 | all-reduce | flops 8192 | bytes 65536 | tf_op jit(solution)/shard_map/psum | solution.py:44
  852.5 0.9 multiply_reduce_fusion
  853.4 96.9 %psum.47 = f32[64]{0:T(128)S(1)} all-reduce(f32[64]{0:T(128)S(1)} %multiply_reduce_fusion), channel_id=1, replica_groups=mesh['samp'=32,'feat'=8] {'samp'}, use_global_device_ids=true, to_apply=%region_10.0 | all-reduce | flops 64 | bytes 512 | tf_op jit(solution)/shard_map/psum | solution.py:45
  950.3 1.5 multiply_subtract_fusion
  (13 shorter events, 0.2 us)
Async XLA Ops:
  7.2 1.2 copy-start
  7.2 106.1 %all-gather.4.cloned.1.call-start = ((), (), s32[]{:S(2)}) async-start(), calls=%async_computation.1 | async-start | bytes 9437184 | tf_op jit(solution)/shard_map/all_gather | solution.py:19
  8.4 104.8 %copy-start.1 = (bf16[1024,64]{0,1:T(8,128)(2,1)S(1)}, bf16[1024,64]{0,1:T(8,128)(2,1)}, u32[]{:S(2)}) copy-start(bf16[1024,64]{0,1:T(8,128)(2,1)} %param.7) | copy-start | bytes 393220
  17.6 394.0 %reduce-scatter.2.cloned.1.call-start = ((), (), s32[]{:S(2)}) async-start(), calls=%async_computation.2 | async-start | bytes 9732096 | tf_op jit(solution)/shard_map/reduce_scatter | solution.py:22
  123.2 372.0 %all-gather.6.cloned.1.call-start = ((), (), s32[]{:S(2)}) async-start(), calls=%async_computation.3 | async-start | bytes 1081344 | tf_op jit(solution)/shard_map/all_gather | solution.py:41
  413.1 414.0 %all-gather.8.cloned.1.call-start = ((), (), s32[]{:S(2)}) async-start(), calls=%async_computation.4 | async-start | bytes 1081344 | tf_op jit(solution)/shard_map/all_gather | solution.py:41
Sparse Core Ops, SparseCore 0:
  17.8 95.4 all-gather.3
  123.3 288.3 reduce-scatter.1
  416.0 79.1 all-gather.5
  715.6 111.4 all-gather.7
where the time goes:
time: 974 us; the launch traced here: 958 us
  waiting for transfers between devices  576 us (59%)
  blocking collectives  337 us (35%)
  matrix products  21.7 us (2%)
  between operations  13.8 us (1%)
    reduce_scatter x1, waiting for transfers between devices, on_device(): lax.psum_scatter(lax.dot_general(features_all, joined, inner, preferred_e...  288 us
    all_gather x2, waiting for transfers between devices, on_device(): gathered = lax.all_gather(direction, 'samp', axis=0, tiled=True)  192 us
    psum x2, blocking collectives, squares(): return lax.psum(jnp.sum(vector * vector, axis=0), 'samp')  192 us
    psum x1, blocking collectives, on_device(): curve = lax.psum(jnp.sum(direction * image, axis=0), 'samp')  96.9 us
    all_gather x1, waiting for transfers between devices, on_device(): features_all = lax.all_gather(local_feats, 'feat', axis=1, tiled=True)  95.6 us
    psum x2, blocking collectives, on_device(): image = lax.psum(partial_value, 'feat') + RIDGE * direction  48.3 us
  transfers between devices with their start and end apart: 4, of which 4 were waited for; matrix products, arithmetic and copies ran while one was open for 0% of the time, Pallas kernels for 0%

commit v1 on v0

v1 whole, which is shorter than its diff:
```python
import math

import jax
import jax.numpy as jnp
from jax import lax
from jax.experimental import pallas as pl
from jax.experimental.pallas import tpu as pltpu
from jax.sharding import PartitionSpec as P

RIDGE = 0.05
ROWS, DEPTH, WIDTH, TARGETS, BLOCK = 1024, 512, 512, 64, 128
TOTAL = 32768
STEP = 512
MESH = pl.DeviceIdType.MESH
SINE = (4.442883014678955, -7.308241367340088, 3.6062889099121094, -0.8457635641098022, 0.10920573770999908)
HIGHEST = lax.Precision.HIGHEST
F32 = jnp.float32


def cosine(angle):
    turns = angle * (0.5 / math.pi)
    f = turns - jnp.round(turns)
    square = f * f
    poly = SINE[-1]
    for coefficient in SINE[-2::-1]:
        poly = poly * square + coefficient
    root = poly * f
    return (1.0 - root * root).astype(jnp.bfloat16)


def remote(src, dst, send_sem, recv_sem, device):
    return pltpu.make_async_remote_copy(
        src_ref=src, dst_ref=dst, send_sem=send_sem, recv_sem=recv_sem, device_id=device, device_id_type=MESH
    )


def greet(peers):
    barrier = pltpu.get_barrier_semaphore()
    for peer in peers:
        pl.semaphore_signal(barrier, inc=1, device_id=peer, device_id_type=MESH)
    pl.semaphore_wait(barrier, len(peers))


def gather_kernel(cnt, tgt, frq, cg, tg, fr, ssem, rsem, fsend, frecv, lsem):
    s, j = lax.axis_index("samp"), lax.axis_index("feat")
    x, c, zl, zh = lax.rem(s, 4), lax.rem(j, 2), lax.div(j, 2), lax.div(s, 16)
    z = zh * 4 + zl
    right = (s - x + lax.rem(x + 1, 4), j)
    left = (s - x + lax.rem(x + 3, 4), j)
    sibling = (s, j + 1 - 2 * c)

    def along_z(dz, core):
        other = lax.rem(z + dz + 8, 8)
        return (lax.div(other, 4) * 16 + lax.rem(s, 16), lax.rem(other, 4) * 2 + core)

    far = 2 - 4 * c
    greet(
        [right, left, sibling]
        + [along_z(dz, core) for dz in (1, -1) for core in (0, 1)]
        + [along_z(far, 0), along_z(far, 1), along_z(-far, c)]
    )

    half = STEP * c
    a_rows, b_rows = pl.ds(pl.multiple_of(half, 256), 256), pl.ds(pl.multiple_of(half + 256, 256), 256)
    a_cols = pl.ds(pl.multiple_of(half, 256), 256)
    b_cols = pl.ds(pl.multiple_of(half + 256, 256), 256)

    def pair(i, src_c, src_t, slot, part, device):
        rows, cols = (a_rows, a_cols) if part == 0 else (b_rows, b_cols)
        return [
            remote(src_c.at[rows], cg.at[slot, rows], ssem.at[2 * i], rsem.at[2 * i], device),
            remote(src_t.at[:, cols], tg.at[slot, :, cols], ssem.at[2 * i + 1], rsem.at[2 * i + 1], device),
        ]

    def twin(i, slot, part):
        other = STEP - half
        rows = pl.ds(pl.multiple_of(other + 256 * part, 256), 256)
        cols = pl.ds(pl.multiple_of(other + 256 * part, 256), 256)
        return [
            remote(cg.at[slot, rows], cg.at[slot, rows], ssem.at[2 * i], rsem.at[2 * i], sibling),
            remote(tg.at[slot, :, cols], tg.at[slot, :, cols], ssem.at[2 * i + 1], rsem.at[2 * i + 1], sibling),
        ]

    to_right = [pair(0, cnt, tgt, 1, 0, right), pair(1, cnt, tgt, 1, 1, right)]
    to_left = [pair(2, cnt, tgt, 2, 0, left), pair(3, cnt, tgt, 2, 1, left)]
    on_right = pair(4, cg.at[1], tg.at[1], 3, 0, right)
    on_left = pair(5, cg.at[2], tg.at[2], 3, 1, left)
    across = {
        (slot, part): pair(6 + 2 * (slot - 1) + part, cg.at[slot], tg.at[slot], slot, part, sibling)
        for slot in (1, 2, 3)
        for part in (0, 1)
    }

    def go(copies):
        for copy in copies:
            copy.start()

    def got(copies):
        for copy in copies:
            copy.wait_recv()

    go(to_right[0])
    go(to_left[1])
    quarter = pl.ds(pl.multiple_of(BLOCK * x, BLOCK), BLOCK)
    mine = pl.ds(pl.multiple_of(BLOCK * j, BLOCK), BLOCK)
    spread = []
    for i, (dz, core) in enumerate([(1, 0), (1, 1), (-1, 0), (-1, 1), (far, 0), (far, 1)]):
        spread.append(remote(frq.at[quarter], fr.at[mine], fsend.at[i], frecv.at[2 * (i // 2) + c], along_z(dz, core)))
    spread.append(remote(frq.at[quarter], fr.at[mine], fsend.at[6], frecv.at[6], sibling))
    go(spread)
    go(to_right[1])
    go(to_left[0])
    local = [
        pltpu.make_async_copy(cnt, cg.at[0], lsem.at[0]),
        pltpu.make_async_copy(tgt, tg.at[0], lsem.at[1]),
        pltpu.make_async_copy(frq.at[quarter], fr.at[mine], lsem.at[2]),
    ]
    go(local)
    got(to_right[0])
    go(on_right)
    go(across[1, 0])
    got(to_left[1])
    go(on_left)
    go(across[2, 1])
    got(to_right[1])
    go(across[1, 1])
    got(to_left[0])
    go(across[2, 0])
    got(on_right)
    go(across[3, 0])
    got(on_left)
    go(across[3, 1])
    for (slot, part), copies in across.items():
        got(twin(6 + 2 * (slot - 1) + part, slot, part))
    for i, (dz, core) in enumerate([(-1, 0), (-1, 1), (1, 0), (1, 1), (-2, 0), (2, 1)]):
        source = along_z(dz, core)
        rows = pl.ds(pl.multiple_of(BLOCK * source[1], BLOCK), BLOCK)
        remote(frq.at[quarter], fr.at[rows], fsend.at[i], frecv.at[2 * (i // 2) + core], source).wait_recv()
    rows = pl.ds(pl.multiple_of(BLOCK * sibling[1], BLOCK), BLOCK)
    remote(frq.at[quarter], fr.at[rows], fsend.at[6], frecv.at[6], sibling).wait_recv()
    for copy in local:
        copy.wait()
    sent = to_right[0] + to_right[1] + to_left[0] + to_left[1] + on_right + on_left + spread
    for copies in across.values():
        sent = sent + copies
    for copy in sent:
        copy.wait_send()


def gather(counters, targets, frequencies):
    bf16 = jnp.bfloat16
    hbm = pl.BlockSpec(memory_space=pl.ANY)
    return pl.pallas_call(
        gather_kernel,
        out_shape=(
            jax.ShapeDtypeStruct((4, ROWS, DEPTH), bf16),
            jax.ShapeDtypeStruct((4, TARGETS, ROWS), bf16),
            jax.ShapeDtypeStruct((8 * BLOCK, DEPTH + 128), bf16),
        ),
        in_specs=[hbm] * 3,
        out_specs=(hbm,) * 3,
        scratch_shapes=[
            pltpu.SemaphoreType.DMA((24,)),
            pltpu.SemaphoreType.DMA((24,)),
            pltpu.SemaphoreType.DMA((7,)),
            pltpu.SemaphoreType.DMA((7,)),
            pltpu.SemaphoreType.DMA((3,)),
        ],
        compiler_params=pltpu.CompilerParams(collective_id=0, has_side_effects=True, vmem_limit_bytes=4 << 20),
        name="gather",
    )(counters, targets, frequencies)


def build_kernel(cnt, tgt, frow, fcol, phase, part, rhs, zrow, gram, right):
    step = pl.program_id(0)
    j = lax.axis_index("feat")

    @pl.when(step == 0)
    def _():
        gram[...] = jnp.zeros_like(gram)
        right[...] = jnp.zeros_like(right)

    nt = (((1,), (1,)), ((), ()))
    rows = cnt[...]
    zcol = cosine(jnp.dot(rows, fcol[...], preferred_element_type=F32) + phase[...].astype(F32))
    mixed = lax.dot_general(frow[:, :DEPTH], rows, nt, preferred_element_type=F32)
    zrow[...] = cosine(mixed + frow[:, DEPTH : DEPTH + 1].astype(F32))
    gram[...] += jnp.dot(zrow[...], zcol, preferred_element_type=F32)
    own = zrow[pl.ds(pl.multiple_of(BLOCK * j, BLOCK), BLOCK), :]
    right[...] += lax.dot_general(tgt[0], own, nt, preferred_element_type=F32)

    @pl.when(step == pl.num_programs(0) - 1)
    def _():
        for block in range(8):
            part[block % 4, block // 4] = gram[block * BLOCK : (block + 1) * BLOCK, :]
        rhs[...] = right[...]


def build(counters, targets, frow, fcol, phases):
    steps = 4 * ROWS // STEP
    per = ROWS // STEP
    whole = lambda shape: pl.BlockSpec(shape, lambda i: (0,) * len(shape))
    return pl.pallas_call(
        build_kernel,
        out_shape=(
            jax.ShapeDtypeStruct((4, 2, BLOCK, WIDTH), F32),
            jax.ShapeDtypeStruct((TARGETS, BLOCK), F32),
        ),
        grid=(steps,),
        in_specs=[
            pl.BlockSpec((STEP, DEPTH), lambda i: (i, 0)),
            pl.BlockSpec((1, TARGETS, STEP), lambda i: (i // per, 0, i % per)),
            whole((8 * BLOCK, DEPTH + 128)),
            whole((DEPTH, WIDTH)),
            whole((1, WIDTH)),
        ],
        out_specs=(whole((4, 2, BLOCK, WIDTH)), whole((TARGETS, BLOCK))),
        scratch_shapes=[
            pltpu.VMEM((8 * BLOCK, STEP), jnp.bfloat16),
            pltpu.VMEM((8 * BLOCK, WIDTH), F32),
            pltpu.VMEM((TARGETS, BLOCK), F32),
        ],
        compiler_params=pltpu.CompilerParams(vmem_limit_bytes=40 << 20),
        name="build",
    )(counters.reshape(4 * ROWS, DEPTH), targets, frow, fcol, phases)


def solve_kernel(
    part, rhs, sol, res, gram,
    ybuf, zsend, zrecv, rh, vj, pout, fb, stat, xb, tot, db, keep, fin,
    ssem, hsem, ysem, zsem, bsem, asem, fsem, xsem, dsem, esem,
):
    s, j = lax.axis_index("samp"), lax.axis_index("feat")
    x, b = lax.rem(s, 4), lax.div(s, 4)
    y, zh = lax.rem(b, 4), lax.div(b, 4)
    diag = b == j
    xmates = [(b * 4 + lax.rem(x + d, 4), j) for d in (1, 2, 3)]
    bothers = [lax.rem(b + e, 8) for e in range(1, 8)]
    bmates = [(o * 4 + x, j) for o in bothers]
    fothers = [lax.rem(j + e, 8) for e in range(1, 8)]
    fmates = [(s, o) for o in fothers]
    dmates = [(o * 4 + x, o) for o in bothers]
    barrier = pltpu.get_barrier_semaphore()
    for peer in xmates + bmates + fmates:
        pl.semaphore_signal(barrier, inc=1, device_id=peer, device_id_type=MESH)

    @pl.when(diag)
    def _():
        for peer in dmates:
            pl.semaphore_signal(barrier, inc=1, device_id=peer, device_id_type=MESH)

    pl.semaphore_wait(barrier, jnp.where(diag, 24, 17))

    count = [0]
    sent, sent_diag = [], []

    def copy(src, dst, recv_sem, device):
        made = remote(src, dst, ssem.at[count[0]], recv_sem, device)
        count[0] += 1
        return made

    def wait(ref, sem):
        remote(ref, ref, ssem.at[0], sem, xmates[0]).wait_recv()

    send_rhs = copy(rhs, rh.at[b], hsem.at[b], (j * 4 + x, j))

    @pl.when(jnp.logical_not(diag))
    def _():
        send_rhs.start()

    for d in (1, 2, 3):
        to = lax.rem(y + d, 4)
        made = copy(part.at[to], ybuf.at[d - 1], ysem.at[d - 1], ((zh * 4 + to) * 4 + x, j))
        made.start()
        sent.append(made)
    for d in (1, 2, 3):
        wait(ybuf.at[d - 1], ysem.at[d - 1])

    def over_y(which):
        total = part[y, which]
        for d in range(3):
            total = total + ybuf[d, which]
        return total

    zsend[...] = over_y(1 - zh)
    send_z = copy(zsend, zrecv, zsem, (((1 - zh) * 4 + y) * 4 + x, j))
    send_z.start()
    sent.append(send_z)
    gram[...] = over_y(zh)

    own = pl.ds(pl.multiple_of(BLOCK * x, BLOCK), BLOCK)

    @pl.when(diag)
    def _():
        total = rhs[...]
        for o in bothers:
            wait(rh.at[o], hsem.at[o])
            total = total + rh[o]
        first = total * (1.0 / math.sqrt(TOTAL))
        keep[0] = first
        vj[0, :, own] = first

    def distribute(it):
        sends = [copy(vj.at[it, :, own], vj.at[it, :, own], bsem.at[it], peer) for peer in bmates]
        sent_diag.extend(sends)

        @pl.when(diag)
        def _():
            for made in sends:
                made.start()

        @pl.when(jnp.logical_not(diag))
        def _():
            wait(vj.at[it, :, own], bsem.at[it])

        for d in (1, 2, 3):
            made = copy(vj.at[it, :, own], vj.at[it, :, own], asem.at[3 * it + d - 1], xmates[d - 1])
            made.start()
            sent.append(made)

    def collect(it):
        for d in (1, 2, 3):
            slot = pl.ds(pl.multiple_of(BLOCK * lax.rem(x + 4 - d, 4), BLOCK), BLOCK)
            wait(vj.at[it, :, slot], asem.at[3 * it + d - 1])

    sent_off = [send_rhs]

    def multiply(it):
        pout[it] = lax.dot_general(
            vj[it], gram[...], (((1,), (1,)), ((), ())), precision=HIGHEST, preferred_element_type=F32
        )
        made = copy(pout.at[it], fb.at[it, j], fsem.at[8 * it + j], (s, b))
        sent_off.append(made)

        @pl.when(jnp.logical_not(diag))
        def _():
            made.start()

    def image(it, vector):
        total = pout[it] + RIDGE * vector
        for o in fothers:
            wait(fb.at[it, o], fsem.at[8 * it + o])
            total = total + fb[it, o]
        return total

    def columns(index):
        return jnp.sum(tot[index], axis=1, keepdims=True)

    planes = [pl.ds(0, 2), pl.ds(2, 1), pl.ds(3, 1)]
    x_sends = [
        [copy(stat.at[p], xb.at[d, p], xsem.at[3 * k + d], xmates[d]) for d in range(3)] for k, p in enumerate(planes)
    ]
    d_sends = [
        [copy(tot.at[p], db.at[e, p], dsem.at[7 * k + e], dmates[e]) for e in range(7)] for k, p in enumerate(planes)
    ]
    for group in x_sends + d_sends:
        sent_diag.extend(group)

    def sum_start(k):
        for made in x_sends[k]:
            made.start()

    def sum_finish(k):
        p = planes[k]
        total = stat[p]
        for d in range(3):
            wait(xb.at[d, p], xsem.at[3 * k + d])
            total = total + xb[d, p]
        tot[p] = total
        for made in d_sends[k]:
            made.start()
        for e in range(7):
            wait(db.at[e, p], dsem.at[7 * k + e])
            total = total + db[e, p]
        for made in d_sends[k]:
            made.wait_send()
        tot[p] = total

    distribute(0)
    collect(0)
    wait(zrecv, zsem)
    gram[...] = (gram[...] + zrecv[...]) * (1.0 / TOTAL)
    multiply(0)

    @pl.when(diag)
    def _():
        first = keep[0]
        w1 = image(0, first)
        keep[1] = w1
        vj[1, :, own] = w1
        stat[0] = first * first
        stat[1] = first * w1

    distribute(1)

    @pl.when(diag)
    def _():
        sum_start(0)

    collect(1)
    multiply(1)

    final = [copy(fin, fin, esem, peer) for peer in fmates]
    sent_diag.extend(final)

    @pl.when(diag)
    def _():
        sum_finish(0)
        first, w1 = keep[0], keep[1]
        rr0 = columns(0)
        a0 = rr0 / columns(1)
        r1 = first - a0 * w1
        stat[2] = r1 * r1
        sum_start(1)
        sum_finish(1)
        rr1 = columns(2)
        b0 = rr1 / rr0
        d1 = r1 + b0 * first
        w2 = image(1, w1)
        image1 = (w1 - a0 * w2) + b0 * w1
        stat[3] = d1 * image1
        sum_start(2)
        sum_finish(2)
        a1 = rr1 / columns(3)
        fin[0] = a0 * first + a1 * d1
        fin[1] = r1 - a1 * image1
        for made in final:
            made.start()

    @pl.when(jnp.logical_not(diag))
    def _():
        wait(fin, esem)

    sol[...] = fin[0]
    res[...] = fin[1]
    for made in sent:
        made.wait_send()

    waited = [made for group in d_sends for made in group]

    @pl.when(diag)
    def _():
        for made in sent_diag:
            if not any(made is other for other in waited):
                made.wait_send()

    @pl.when(jnp.logical_not(diag))
    def _():
        for made in sent_off:
            made.wait_send()


def solve(part, rhs):
    vmem = pl.BlockSpec(memory_space=pltpu.VMEM)
    dma = pltpu.SemaphoreType.DMA
    vector = (TARGETS, BLOCK)
    return pl.pallas_call(
        solve_kernel,
        out_shape=(
            jax.ShapeDtypeStruct(vector, F32),
            jax.ShapeDtypeStruct(vector, F32),
            jax.ShapeDtypeStruct((BLOCK, WIDTH), F32),
        ),
        in_specs=[vmem] * 2,
        out_specs=(vmem,) * 3,
        scratch_shapes=[
            pltpu.VMEM((3, 2, BLOCK, WIDTH), F32),
            pltpu.VMEM((BLOCK, WIDTH), F32),
            pltpu.VMEM((BLOCK, WIDTH), F32),
            pltpu.VMEM((8,) + vector, F32),
            pltpu.VMEM((2, TARGETS, WIDTH), F32),
            pltpu.VMEM((2,) + vector, F32),
            pltpu.VMEM((2, 8) + vector, F32),
            pltpu.VMEM((4,) + vector, F32),
            pltpu.VMEM((3, 4) + vector, F32),
            pltpu.VMEM((4,) + vector, F32),
            pltpu.VMEM((7, 4) + vector, F32),
            pltpu.VMEM((2,) + vector, F32),
            pltpu.VMEM((2,) + vector, F32),
            dma((72,)),
            dma((8,)),
            dma((3,)),
            dma,
            dma((2,)),
            dma((6,)),
            dma((16,)),
            dma((9,)),
            dma((21,)),
            dma,
        ],
        compiler_params=pltpu.CompilerParams(collective_id=1, has_side_effects=True, vmem_limit_bytes=24 << 20),
        name="solve",
    )(part, rhs)


def on_device(counters, frequencies, phases, targets):
    columns = jnp.concatenate([frequencies.T, jnp.broadcast_to(phases.T, (WIDTH, 128))], axis=1)
    all_counters, all_targets, rows = gather(counters, targets.T, columns)
    part, rhs = build(all_counters, all_targets, rows, frequencies, phases)
    solution, residual, gram = solve(part, rhs)
    return solution.T, residual.T, gram


def solution(mesh):
    return jax.shard_map(
        on_device,
        mesh=mesh,
        in_specs=(P("samp", None), P(None, "feat"), P(None, "feat"), P("samp", None)),
        out_specs=(P("samp", None), P("samp", None), P("samp", "feat")),
        check_vma=False,
    )
```

time: 974 us -> 154 us (0.16); the launches traced: 958 us -> 151 us
  waiting for transfers between devices: 576 us -> 0 us
  blocking collectives: 337 us -> 0 us
  Pallas kernels: 0 us -> 146 us
  matrix products: 21.7 us -> 0 us
  between operations: 13.8 us -> 0.74 us
    psum x5 -> x0, blocking collectives: 337 us -> none  [the longest x2 192 us: squares(): return lax.psum(jnp.sum(vector * vector, axis=0), 'samp')]
    reduce_scatter x1 -> x0, waiting for transfers between devices: 288 us -> none  [on_device(): lax.psum_scatter(lax.dot_general(features_all, joined, inner, preferred_e...]
    all_gather x3 -> x0, waiting for transfers between devices: 287 us -> none  [the longest x2 192 us: on_device(): gathered = lax.all_gather(direction, 'samp', axis=0, tiled=True)]
    pallas_call x0 -> x3, Pallas kernels: none -> 146 us  [the longest x1 91.1 us: solve(): pl.pallas_call(solve_kernel, out_shape=(jax.ShapeDtypeStruct(vector, F32)...]
    dot_general x4 -> x0, matrix products: 21.7 us -> none  [the longest x1 9.93 us: on_device(): lax.dot_general(features_all, joined, inner, preferred_element_type=jnp.f...]
  transfers between devices with their start and end apart: 4 -> 0, of which waited for: 4 -> 0; matrix products, arithmetic and copies ran while one was open for 0% -> 0% of each run, Pallas kernels for 0% -> 0%
where the time goes in v1:
time: 154 us; the launch traced here: 151 us
  Pallas kernels  146 us (95%)
  local copies, waits for them, and re-layouts  3.34 us (2%)
    pallas_call x1, Pallas kernels, solve(): pl.pallas_call(solve_kernel, out_shape=(jax.ShapeDtypeStruct(vector, F32)...  91.1 us
    pallas_call x1, Pallas kernels, gather(): pl.pallas_call(gather_kernel, out_shape=(jax.ShapeDtypeStruct((4, ROWS, D...  32.9 us
    pallas_call x1, Pallas kernels, build(): pl.pallas_call(build_kernel, out_shape=(jax.ShapeDtypeStruct((4, 2, BLOCK...  21.8 us
    unnamed x12, local copies, waits for them, and re-layouts  3.21 us

profile of v1, /device:TPU:1, one launch (start us, length us, event | category | flops | bytes accessed | tf_op | source)
XLA Modules:
  0.0 150.7 jit_solution(6389273342468065565)
XLA Ops:
  0.6 0.0 copy-start.2
  0.6 0.0 copy-start.1
  0.6 0.8 reduce
  1.4 0.1 broadcast_in_dim.8
  1.6 1.3 copy.7
  2.8 0.0 copy-start
  2.9 0.0 copy-start.3
  2.9 0.1 pad_maximum_fusion.frq
  2.9 0.0 copy-done.2
  2.9 0.0 copy-done.1
  3.0 32.9 %gather.1 = (bf16[4,1024,512]{2,1,0:T(8,128)(2,1)S(1)}, bf16[4,64,1024]{2,1,0:T(8,128)(2,1)S(1)}, bf16[1024,640]{1,0:T(8,128)(2,1)S(1)}) custom-call(bf16[1024,512]{1,0:T(8,128)(2,1)S(1)} %copy-done.1, bf16[64,1024]{1,0:T(8,128)(2,1)S(1)} %bitcast.6, bf16[512,640]{1,0:T(8,128)(2,1)S(1)} %pad_maximum_fusion.frq), custom_call_target="tpu_custom_call" | custom-call | tf_op jit(solution)/shard_map/gather/pallas_call | solution.py:153
  35.9 0.0 copy-done
  35.9 0.0 copy-done.3
  35.9 21.8 %build.1 = (f32[4,2,128,512]{3,2,1,0:T(8,128)S(1)}, f32[64,128]{1,0:T(8,128)S(1)}) custom-call(bf16[4096,512]{1,0:T(8,128)(2,1)S(1)} %bitcast.5, bf16[4,64,1024]{2,1,0:T(8,128)(2,1)S(1)} %get-tuple-element.12.tgt, bf16[1024,640]{1,0:T(8,128)(2,1)S(1)} %get-tuple-element.13.frow, bf16[512,512]{1,0:T(8,128)(2,1)S(1)} %copy-done, bf16[1,512]{1,0:T(2,128)(2,1)S(1)} %copy-done.3), custom_call_target="tpu_custom_call" | custom-call | tf_op jit(solution)/shard_map/build/pallas_call | solution.py:203
  57.7 91.1 %solve.1 = (f32[64,128]{1,0:T(8,128)S(1)}, f32[64,128]{1,0:T(8,128)S(1)}, f32[128,512]{1,0:T(8,128)S(1)}) custom-call(f32[4,2,128,512]{3,2,1,0:T(8,128)S(1)} %get-tuple-element.14.part, f32[64,128]{1,0:T(8,128)S(1)} %get-tuple-element.15.rhs), custom_call_target="tpu_custom_call" | custom-call | tf_op jit(solution)/shard_map/solve/pallas_call | solution.py:457
  148.8 0.6 copy.11
  149.4 0.6 copy.12
  150.0 0.7 copy.13
Async XLA Ops:
  0.6 2.3 %copy-start.2 = (bf16[1024,64]{0,1:T(8,128)(2,1)S(1)}, bf16[1024,64]{0,1:T(8,128)(2,1)}, u32[]{:S(2)}) copy-start(bf16[1024,64]{0,1:T(8,128)(2,1)} %param.7) | copy-start | bytes 393220
  0.6 2.3 %copy-start.1 = (bf16[1024,512]{1,0:T(8,128)(2,1)S(1)}, bf16[1024,512]{1,0:T(8,128)(2,1)}, u32[]{:S(2)}) copy-start(bf16[1024,512]{1,0:T(8,128)(2,1)} %cnt.1) | copy-start | bytes 3145732
  2.8 33.0 %copy-start = (bf16[512,512]{1,0:T(8,128)(2,1)S(1)}, bf16[512,512]{1,0:T(8,128)(2,1)}, u32[]{:S(2)}) copy-start(bf16[512,512]{1,0:T(8,128)(2,1)} %fcol.1) | copy-start | bytes 1572868
  2.9 33.0 %copy-start.3 = (bf16[1,512]{1,0:T(2,128)(2,1)S(1)}, bf16[1,512]{1,0:T(2,128)(2,1)}, u32[]{:S(2)}) copy-start(bf16[1,512]{1,0:T(2,128)(2,1)} %phase.1) | copy-start | bytes 3076

commit v2 on v1

--- a/solution.py
+++ b/solution.py
@@ -227,233 +227,216 @@
 
 def solve_kernel(
     part, rhs, sol, res, gram,
-    ybuf, zsend, zrecv, rh, vj, pout, fb, stat, xb, tot, db, keep, fin,
-    ssem, hsem, ysem, zsem, bsem, asem, fsem, xsem, dsem, esem,
+    ybuf, zsend, zrecv, gother, rh, rj, vj, first, fb, xb, db, w1buf, fin,
+    ssem, hsem, rsem, osem, psem, ysem, zsem, gsem, fsem, tsem, xsem, dsem, esem,
 ):
     s, j = lax.axis_index("samp"), lax.axis_index("feat")
     x, b = lax.rem(s, 4), lax.div(s, 4)
     y, zh = lax.rem(b, 4), lax.div(b, 4)
+    c, zl = lax.rem(j, 2), lax.div(j, 2)
     diag = b == j
-    xmates = [(b * 4 + lax.rem(x + d, 4), j) for d in (1, 2, 3)]
+    sibling = (s, j + 1 - 2 * c)
+    xothers = [lax.rem(x + d, 4) for d in (1, 2, 3)]
+    xmates = [(b * 4 + o, j) for o in xothers]
     bothers = [lax.rem(b + e, 8) for e in range(1, 8)]
     bmates = [(o * 4 + x, j) for o in bothers]
     fothers = [lax.rem(j + e, 8) for e in range(1, 8)]
     fmates = [(s, o) for o in fothers]
-    dmates = [(o * 4 + x, o) for o in bothers]
+    zothers = [lax.rem(zl + d, 4) for d in (1, 2, 3)]
+    zmates = [(s, o * 2 + c) for o in zothers]
+    spread_to = [((h * 4 + zl) * 4 + o, lax.div(b, 2) * 2 + c) for h in (0, 1) for o in range(4)]
+    spread_from = [((zl * 2 + h) * 4 + o, y * 2 + c) for h in (0, 1) for o in range(4)]
+    loop = jnp.logical_and(lax.div(b, 2) == zl, y == zl)
+
     barrier = pltpu.get_barrier_semaphore()
     for peer in xmates + bmates + fmates:
         pl.semaphore_signal(barrier, inc=1, device_id=peer, device_id_type=MESH)
-
-    @pl.when(diag)
-    def _():
-        for peer in dmates:
+    for peer in spread_from:
+
+        @pl.when(peer[0] * 8 + peer[1] != s * 8 + j)
+        def _(peer=peer):
             pl.semaphore_signal(barrier, inc=1, device_id=peer, device_id_type=MESH)
 
-    pl.semaphore_wait(barrier, jnp.where(diag, 24, 17))
+    pl.semaphore_wait(barrier, jnp.where(loop, 24, 25))
 
     count = [0]
-    sent, sent_diag = [], []
-
-    def copy(src, dst, recv_sem, device):
+    sent = []
+
+    def copy(src, dst, recv_sem, device, when=None):
         made = remote(src, dst, ssem.at[count[0]], recv_sem, device)
         count[0] += 1
-        return made
+        sent.append((made, when))
+        if when is None:
+            made.start()
+        else:
+            pl.when(when)(made.start)
 
     def wait(ref, sem):
-        remote(ref, ref, ssem.at[0], sem, xmates[0]).wait_recv()
-
-    send_rhs = copy(rhs, rh.at[b], hsem.at[b], (j * 4 + x, j))
+        remote(ref, ref, ssem.at[0], sem, sibling).wait_recv()
+
+    def lanes(block, size=BLOCK):
+        return pl.ds(pl.multiple_of(block * size, size), size)
+
+    half, other_half = pl.ds(32 * c, 32), pl.ds(32 * (1 - c), 32)
+
+    rh[b] = rhs[...]
+    for o, peer in zip(bothers, bmates):
+        copy(rh.at[b], rh.at[b], hsem.at[b], peer)
+    for d in (1, 2, 3):
+        to = lax.rem(y + d, 4)
+        copy(part.at[to, 1 - zh], ybuf.at[d - 1, 0], ysem.at[d - 1], ((zh * 4 + to) * 4 + x, j))
+    for d in (1, 2, 3):
+        to = lax.rem(y + d, 4)
+        copy(part.at[to, zh], ybuf.at[d - 1, 1], ysem.at[d + 2], ((zh * 4 + to) * 4 + x, j))
+
+    for o in bothers:
+        wait(rh.at[o], hsem.at[o])
+    total = rh[0]
+    for o in range(1, 8):
+        total = total + rh[o]
+    total = total * (1.0 / math.sqrt(TOTAL))
+    rj[:, lanes(x)] = total
+    for peer in xmates:
+        copy(rj.at[:, lanes(x)], rj.at[:, lanes(x)], rsem.at[x], peer)
+    for core in (0, 1):
+
+        @pl.when(jnp.logical_and(diag, c == core))
+        def _(core=core):
+            first[...] = total[32 * core : 32 * core + 32]
+
+    for o, peer in zip(fothers, fmates):
+        copy(rj.at[pl.ds(32 * lax.rem(o, 2), 32), lanes(x)], first, psem, peer, diag)
+    for o in xothers:
+        wait(rj.at[:, lanes(o)], rsem.at[o])
+    for core in (0, 1):
+
+        @pl.when(c == core)
+        def _(core=core):
+            vj[0, :, core * WIDTH : (core + 1) * WIDTH] = rj[32 * core : 32 * core + 32, :]
+
+    copy(rj.at[other_half, :], vj.at[0, :, lanes(c, WIDTH)], osem, sibling)
+
+    def over_y(which, slot):
+        total = part[y, which]
+        for d in range(3):
+            wait(ybuf.at[d, slot], ysem.at[3 * slot + d])
+            total = total + ybuf[d, slot]
+        return total
+
+    zsend[...] = over_y(1 - zh, 0)
+    copy(zsend, zrecv, zsem, (((1 - zh) * 4 + y) * 4 + x, j))
+    gram[...] = over_y(zh, 1)
+    wait(vj.at[0, :, lanes(1 - c, WIDTH)], osem)
 
     @pl.when(jnp.logical_not(diag))
     def _():
-        send_rhs.start()
-
-    for d in (1, 2, 3):
-        to = lax.rem(y + d, 4)
-        made = copy(part.at[to], ybuf.at[d - 1], ysem.at[d - 1], ((zh * 4 + to) * 4 + x, j))
-        made.start()
-        sent.append(made)
-    for d in (1, 2, 3):
-        wait(ybuf.at[d - 1], ysem.at[d - 1])
-
-    def over_y(which):
-        total = part[y, which]
-        for d in range(3):
-            total = total + ybuf[d, which]
-        return total
-
-    zsend[...] = over_y(1 - zh)
-    send_z = copy(zsend, zrecv, zsem, (((1 - zh) * 4 + y) * 4 + x, j))
-    send_z.start()
-    sent.append(send_z)
-    gram[...] = over_y(zh)
-
-    own = pl.ds(pl.multiple_of(BLOCK * x, BLOCK), BLOCK)
-
-    @pl.when(diag)
-    def _():
-        total = rhs[...]
-        for o in bothers:
-            wait(rh.at[o], hsem.at[o])
-            total = total + rh[o]
-        first = total * (1.0 / math.sqrt(TOTAL))
-        keep[0] = first
-        vj[0, :, own] = first
-
-    def distribute(it):
-        sends = [copy(vj.at[it, :, own], vj.at[it, :, own], bsem.at[it], peer) for peer in bmates]
-        sent_diag.extend(sends)
-
-        @pl.when(diag)
-        def _():
-            for made in sends:
-                made.start()
-
-        @pl.when(jnp.logical_not(diag))
-        def _():
-            wait(vj.at[it, :, own], bsem.at[it])
-
-        for d in (1, 2, 3):
-            made = copy(vj.at[it, :, own], vj.at[it, :, own], asem.at[3 * it + d - 1], xmates[d - 1])
-            made.start()
-            sent.append(made)
-
-    def collect(it):
-        for d in (1, 2, 3):
-            slot = pl.ds(pl.multiple_of(BLOCK * lax.rem(x + 4 - d, 4), BLOCK), BLOCK)
-            wait(vj.at[it, :, slot], asem.at[3 * it + d - 1])
-
-    sent_off = [send_rhs]
-
-    def multiply(it):
-        pout[it] = lax.dot_general(
-            vj[it], gram[...], (((1,), (1,)), ((), ())), precision=HIGHEST, preferred_element_type=F32
-        )
-        made = copy(pout.at[it], fb.at[it, j], fsem.at[8 * it + j], (s, b))
-        sent_off.append(made)
-
-        @pl.when(jnp.logical_not(diag))
-        def _():
-            made.start()
-
-    def image(it, vector):
-        total = pout[it] + RIDGE * vector
-        for o in fothers:
-            wait(fb.at[it, o], fsem.at[8 * it + o])
-            total = total + fb[it, o]
-        return total
-
-    def columns(index):
-        return jnp.sum(tot[index], axis=1, keepdims=True)
-
-    planes = [pl.ds(0, 2), pl.ds(2, 1), pl.ds(3, 1)]
-    x_sends = [
-        [copy(stat.at[p], xb.at[d, p], xsem.at[3 * k + d], xmates[d]) for d in range(3)] for k, p in enumerate(planes)
-    ]
-    d_sends = [
-        [copy(tot.at[p], db.at[e, p], dsem.at[7 * k + e], dmates[e]) for e in range(7)] for k, p in enumerate(planes)
-    ]
-    for group in x_sends + d_sends:
-        sent_diag.extend(group)
-
-    def sum_start(k):
-        for made in x_sends[k]:
-            made.start()
-
-    def sum_finish(k):
-        p = planes[k]
-        total = stat[p]
-        for d in range(3):
-            wait(xb.at[d, p], xsem.at[3 * k + d])
-            total = total + xb[d, p]
-        tot[p] = total
-        for made in d_sends[k]:
-            made.start()
-        for e in range(7):
-            wait(db.at[e, p], dsem.at[7 * k + e])
-            total = total + db[e, p]
-        for made in d_sends[k]:
-            made.wait_send()
-        tot[p] = total
-
-    distribute(0)
-    collect(0)
+        wait(first, psem)
+
     wait(zrecv, zsem)
     gram[...] = (gram[...] + zrecv[...]) * (1.0 / TOTAL)
-    multiply(0)
-
-    @pl.when(diag)
+    copy(gram, gother, gsem, sibling)
+
+    def multiply(it, wait_gram):
+        nt = (((1,), (1,)), ((), ()))
+        own = lax.dot_general(vj[it, :, lanes(c, WIDTH)], gram[...], nt, precision=HIGHEST, preferred_element_type=F32)
+        if wait_gram:
+            wait(gother, gsem)
+        fb[it, zl] = own + lax.dot_general(
+            vj[it, :, lanes(1 - c, WIDTH)], gother[...], nt, precision=HIGHEST, preferred_element_type=F32
+        )
+        for peer in zmates:
+            copy(fb.at[it, zl], fb.at[it, zl], fsem.at[4 * it + zl], peer)
+
+    def image(it, vector):
+        for o in zothers:
+            wait(fb.at[it, o], fsem.at[4 * it + o])
+        return ((fb[it, 0] + fb[it, 1]) + (fb[it, 2] + fb[it, 3])) + RIDGE * vector
+
+    planes = [(0, 2), (2, 1), (3, 1)]
+
+    def sum_start(k, values):
+        p, n = planes[k]
+        for i, value in enumerate(values):
+            xb[x, p + i] = value
+        for peer in xmates:
+            copy(xb.at[x, pl.ds(p, n)], xb.at[x, pl.ds(p, n)], xsem.at[4 * k + x], peer)
+
+    def sum_finish(k):
+        p, n = planes[k]
+        for o in xothers:
+            wait(xb.at[o, pl.ds(p, n)], xsem.at[4 * k + o])
+        for i in range(p, p + n):
+            db[b, i] = (xb[0, i] + xb[1, i]) + (xb[2, i] + xb[3, i])
+        for peer in bmates:
+            copy(db.at[b, pl.ds(p, n)], db.at[b, pl.ds(p, n)], dsem.at[8 * k + b], peer)
+        for o in bothers:
+            wait(db.at[o, pl.ds(p, n)], dsem.at[8 * k + o])
+        out = []
+        for i in range(p, p + n):
+            total = db[0, i]
+            for o in range(1, 8):
+                total = total + db[o, i]
+            out.append(jnp.sum(total, axis=1, keepdims=True))
+        return out
+
+    multiply(0, True)
+    r0 = first[...]
+    w1 = image(0, r0)
+    w1buf[...] = w1
+    place = lax.rem(b, 2) * 4 + x
+    for peer in spread_to:
+        copy(w1buf, vj.at[1, :, lanes(place)], tsem.at[place], peer, peer[0] * 8 + peer[1] != s * 8 + j)
+
+    @pl.when(loop)
     def _():
-        first = keep[0]
-        w1 = image(0, first)
-        keep[1] = w1
-        vj[1, :, own] = w1
-        stat[0] = first * first
-        stat[1] = first * w1
-
-    distribute(1)
-
-    @pl.when(diag)
-    def _():
-        sum_start(0)
-
-    collect(1)
-    multiply(1)
-
-    final = [copy(fin, fin, esem, peer) for peer in fmates]
-    sent_diag.extend(final)
-
-    @pl.when(diag)
-    def _():
-        sum_finish(0)
-        first, w1 = keep[0], keep[1]
-        rr0 = columns(0)
-        a0 = rr0 / columns(1)
-        r1 = first - a0 * w1
-        stat[2] = r1 * r1
-        sum_start(1)
-        sum_finish(1)
-        rr1 = columns(2)
-        b0 = rr1 / rr0
-        d1 = r1 + b0 * first
-        w2 = image(1, w1)
-        image1 = (w1 - a0 * w2) + b0 * w1
-        stat[3] = d1 * image1
-        sum_start(2)
-        sum_finish(2)
-        a1 = rr1 / columns(3)
-        fin[0] = a0 * first + a1 * d1
-        fin[1] = r1 - a1 * image1
-        for made in final:
-            made.start()
-
-    @pl.when(jnp.logical_not(diag))
-    def _():
-        wait(fin, esem)
-
+        vj[1, :, lanes(place)] = w1
+
+    sum_start(0, [r0 * r0, r0 * w1])
+    for i, peer in enumerate(spread_from):
+
+        @pl.when(peer[0] * 8 + peer[1] != s * 8 + j)
+        def _(i=i):
+            wait(vj.at[1, :, BLOCK * i : BLOCK * (i + 1)], tsem.at[i])
+
+    multiply(1, False)
+    rr0, curve0 = sum_finish(0)
+    a0 = rr0 / curve0
+    r1 = r0 - a0 * w1
+    sum_start(1, [r1 * r1])
+    (rr1,) = sum_finish(1)
+    b0 = rr1 / rr0
+    d1 = r1 + b0 * r0
+    w2 = image(1, w1)
+    image1 = (w1 - a0 * w2) + b0 * w1
+    sum_start(2, [d1 * image1])
+    (curve1,) = sum_finish(2)
+    a1 = rr1 / curve1
+    for core in (0, 1):
+
+        @pl.when(c == core)
+        def _(core=core):
+            fin[0, 32 * core : 32 * core + 32] = a0 * r0 + a1 * d1
+            fin[1, 32 * core : 32 * core + 32] = r1 - a1 * image1
+
+    copy(fin.at[:, half], fin.at[:, half], esem, sibling)
+    wait(fin.at[:, other_half], esem)
     sol[...] = fin[0]
     res[...] = fin[1]
-    for made in sent:
-        made.wait_send()
-
-    waited = [made for group in d_sends for made in group]
-
-    @pl.when(diag)
-    def _():
-        for made in sent_diag:
-            if not any(made is other for other in waited):
-                made.wait_send()
-
-    @pl.when(jnp.logical_not(diag))
-    def _():
-        for made in sent_off:
+    for made, when in sent:
+        if when is None:
             made.wait_send()
+        else:
+            pl.when(when)(made.wait_send)
 
 
 def solve(part, rhs):
     vmem = pl.BlockSpec(memory_space=pltpu.VMEM)
     dma = pltpu.SemaphoreType.DMA
-    vector = (TARGETS, BLOCK)
+    vector, some = (TARGETS, BLOCK), (TARGETS // 2, BLOCK)
+    shapes = [
+        (3, 2, BLOCK, WIDTH), (BLOCK, WIDTH), (BLOCK, WIDTH), (BLOCK, WIDTH), (8,) + vector, (TARGETS, WIDTH),
+        (2, TARGETS // 2, 2 * WIDTH), some, (2, 4) + some, (4, 4) + some, (8, 4) + some, some, (2,) + vector,
+    ]
     return pl.pallas_call(
         solve_kernel,
         out_shape=(
@@ -463,30 +446,10 @@
         ),
         in_specs=[vmem] * 2,
         out_specs=(vmem,) * 3,
-        scratch_shapes=[
-            pltpu.VMEM((3, 2, BLOCK, WIDTH), F32),
-            pltpu.VMEM((BLOCK, WIDTH), F32),
-            pltpu.VMEM((BLOCK, WIDTH), F32),
-            pltpu.VMEM((8,) + vector, F32),
-            pltpu.VMEM((2, TARGETS, WIDTH), F32),
-            pltpu.VMEM((2,) + vector, F32),
-            pltpu.VMEM((2, 8) + vector, F32),
-            pltpu.VMEM((4,) + vector, F32),
-            pltpu.VMEM((3, 4) + vector, F32),
-            pltpu.VMEM((4,) + vector, F32),
-            pltpu.VMEM((7, 4) + vector, F32),
-            pltpu.VMEM((2,) + vector, F32),
-            pltpu.VMEM((2,) + vector, F32),
-            dma((72,)),
-            dma((8,)),
-            dma((3,)),
-            dma,
-            dma((2,)),
-            dma((6,)),
-            dma((16,)),
-            dma((9,)),
-            dma((21,)),
-            dma,
+        scratch_shapes=[pltpu.VMEM(shape, F32) for shape in shapes]
+        + [
+            dma((80,)), dma((8,)), dma((4,)), dma, dma, dma((6,)), dma, dma, dma((8,)), dma((8,)),
+            dma((12,)), dma((24,)), dma,
         ],
         compiler_params=pltpu.CompilerParams(collective_id=1, has_side_effects=True, vmem_limit_bytes=24 << 20),
         name="solve",

time: 154 us -> 146 us (0.948); the launches traced: 151 us -> 146 us
  Pallas kernels: 146 us -> 141 us
    pallas_call x1, Pallas kernels: 91.1 us -> 86 us  [solve(): pl.pallas_call(solve_kernel, out_shape=(jax.ShapeDtypeStruct(vector, F32)...]
where the time goes in v2:
time: 146 us
  Pallas kernels  141 us (97%)
  local copies, waits for them, and re-layouts  3.34 us (2%)
    pallas_call x1, Pallas kernels, solve(): pl.pallas_call(solve_kernel, out_shape=(jax.ShapeDtypeStruct(vector, F32)...  86 us
    pallas_call x1, Pallas kernels, gather(): pl.pallas_call(gather_kernel, out_shape=(jax.ShapeDtypeStruct((4, ROWS, D...  32.9 us
    pallas_call x1, Pallas kernels, build(): pl.pallas_call(build_kernel, out_shape=(jax.ShapeDtypeStruct((4, 2, BLOCK...  21.8 us
    unnamed x12, local copies, waits for them, and re-layouts  3.21 us

profile of v2, /device:TPU:1, one launch (start us, length us, event | category | flops | bytes accessed | tf_op | source)
XLA Modules:
  0.0 145.6 jit_solution(10546169150893526950)
XLA Ops:
  0.6 0.0 copy-start.2
  0.6 0.0 copy-start.1
  0.6 0.8 reduce
  1.4 0.1 broadcast_in_dim.8
  1.6 1.3 copy.7
  2.8 0.0 copy-start
  2.9 0.0 copy-start.3
  2.9 0.1 pad_maximum_fusion.frq
  2.9 0.0 copy-done.2
  2.9 0.0 copy-done.1
  3.0 32.9 %gather.1 = (bf16[4,1024,512]{2,1,0:T(8,128)(2,1)S(1)}, bf16[4,64,1024]{2,1,0:T(8,128)(2,1)S(1)}, bf16[1024,640]{1,0:T(8,128)(2,1)S(1)}) custom-call(bf16[1024,512]{1,0:T(8,128)(2,1)S(1)} %copy-done.1, bf16[64,1024]{1,0:T(8,128)(2,1)S(1)} %bitcast.6, bf16[512,640]{1,0:T(8,128)(2,1)S(1)} %pad_maximum_fusion.frq), custom_call_target="tpu_custom_call" | custom-call | tf_op jit(solution)/shard_map/gather/pallas_call | solution.py:153
  35.9 0.0 copy-done
  35.9 0.0 copy-done.3
  35.9 21.8 %build.1 = (f32[4,2,128,512]{3,2,1,0:T(8,128)S(1)}, f32[64,128]{1,0:T(8,128)S(1)}) custom-call(bf16[4096,512]{1,0:T(8,128)(2,1)S(1)} %bitcast.5, bf16[4,64,1024]{2,1,0:T(8,128)(2,1)S(1)} %get-tuple-element.12.tgt, bf16[1024,640]{1,0:T(8,128)(2,1)S(1)} %get-tuple-element.13.frow, bf16[512,512]{1,0:T(8,128)(2,1)S(1)} %copy-done, bf16[1,512]{1,0:T(2,128)(2,1)S(1)} %copy-done.3), custom_call_target="tpu_custom_call" | custom-call | tf_op jit(solution)/shard_map/build/pallas_call | solution.py:203
  57.7 86.0 %solve.1 = (f32[64,128]{1,0:T(8,128)S(1)}, f32[64,128]{1,0:T(8,128)S(1)}, f32[128,512]{1,0:T(8,128)S(1)}) custom-call(f32[4,2,128,512]{3,2,1,0:T(8,128)S(1)} %get-tuple-element.14.part, f32[64,128]{1,0:T(8,128)S(1)} %get-tuple-element.15.rhs), custom_call_target="tpu_custom_call" | custom-call | tf_op jit(solution)/shard_map/solve/pallas_call | solution.py:440
  143.7 0.6 copy.11
  144.3 0.6 copy.12
  144.9 0.7 copy.13
Async XLA Ops:
  0.6 2.3 %copy-start.2 = (bf16[1024,64]{0,1:T(8,128)(2,1)S(1)}, bf16[1024,64]{0,1:T(8,128)(2,1)}, u32[]{:S(2)}) copy-start(bf16[1024,64]{0,1:T(8,128)(2,1)} %param.7) | copy-start | bytes 393220
  0.6 2.3 %copy-start.1 = (bf16[1024,512]{1,0:T(8,128)(2,1)S(1)}, bf16[1024,512]{1,0:T(8,128)(2,1)}, u32[]{:S(2)}) copy-start(bf16[1024,512]{1,0:T(8,128)(2,1)} %cnt.1) | copy-start | bytes 3145732
  2.8 33.0 %copy-start = (bf16[512,512]{1,0:T(8,128)(2,1)S(1)}, bf16[512,512]{1,0:T(8,128)(2,1)}, u32[]{:S(2)}) copy-start(bf16[512,512]{1,0:T(8,128)(2,1)} %fcol.1) | copy-start | bytes 1572868
  2.9 33.0 %copy-start.3 = (bf16[1,512]{1,0:T(2,128)(2,1)S(1)}, bf16[1,512]{1,0:T(2,128)(2,1)}, u32[]{:S(2)}) copy-start(bf16[1,512]{1,0:T(2,128)(2,1)} %phase.1) | copy-start | bytes 3076

commit v3 on v2

--- a/solution.py
+++ b/solution.py
@@ -227,8 +227,8 @@
 
 def solve_kernel(
     part, rhs, sol, res, gram,
-    ybuf, zsend, zrecv, gother, rh, rj, vj, first, fb, xb, db, w1buf, fin,
-    ssem, hsem, rsem, osem, psem, ysem, zsem, gsem, fsem, tsem, xsem, dsem, esem,
+    ybuf, zsend, zrecv, gother, rh, rj, vj, first, fb, sums, w1buf, fin,
+    ssem, hsem, rsem, osem, psem, ysem, zsem, gsem, fsem, tsem, xsem, esem,
 ):
     s, j = lax.axis_index("samp"), lax.axis_index("feat")
     x, b = lax.rem(s, 4), lax.div(s, 4)
@@ -244,20 +244,32 @@
     fmates = [(s, o) for o in fothers]
     zothers = [lax.rem(zl + d, 4) for d in (1, 2, 3)]
     zmates = [(s, o * 2 + c) for o in zothers]
-    spread_to = [((h * 4 + zl) * 4 + o, lax.div(b, 2) * 2 + c) for h in (0, 1) for o in range(4)]
-    spread_from = [((zl * 2 + h) * 4 + o, y * 2 + c) for h in (0, 1) for o in range(4)]
-    loop = jnp.logical_and(lax.div(b, 2) == zl, y == zl)
+    yothers = [lax.rem(y + d, 4) for d in (1, 2, 3)]
+    ymates = [((zh * 4 + o) * 4 + x, j) for o in yothers]
+    z = zh * 4 + zl
+    rothers = [lax.rem(z + e, 8) for e in range(1, 8)]
+    rmates = [((lax.div(o, 4) * 4 + y) * 4 + x, lax.rem(o, 4) * 2 + c) for o in rothers]
+    across = [((1 - zh) * 16 + y * 4 + x, o * 2 + c) for o in zothers]
+    down = lax.div(b, 2)
+    same = lax.div(zl, 2) == zh
+    near = jnp.where(same, zl == down, zl == 3 * (1 - zh))
+    to_zh = jnp.where(same, zh, 1 - zh)
+    skip = jnp.where(near, 2, 0)
+    spread_to = [((to_zh * 4 + lax.rem(y + skip + d, 4)) * 4 + o, down * 2 + c) for d in (0, 1) for o in range(4)]
+    spread_from = []
+    for h in (0, 1):
+        source_y, source_zh = lax.rem(zl, 2) * 2 + h, lax.div(zl, 2)
+        far = jnp.where(lax.rem(y + 4 - source_y, 4) < 2, 1, 0)
+        inside = zl + far * (1 - 2 * lax.rem(zl, 2))
+        outside = jnp.where(source_zh == 0, 3 - far, far)
+        source_zl = jnp.where(zh == source_zh, inside, outside)
+        spread_from += [((zl * 2 + h) * 4 + o, source_zl * 2 + c) for o in range(4)]
 
     barrier = pltpu.get_barrier_semaphore()
-    for peer in xmates + bmates + fmates:
+    peers = xmates + bmates + fmates + across + spread_from
+    for peer in peers:
         pl.semaphore_signal(barrier, inc=1, device_id=peer, device_id_type=MESH)
-    for peer in spread_from:
-
-        @pl.when(peer[0] * 8 + peer[1] != s * 8 + j)
-        def _(peer=peer):
-            pl.semaphore_signal(barrier, inc=1, device_id=peer, device_id_type=MESH)
-
-    pl.semaphore_wait(barrier, jnp.where(loop, 24, 25))
+    pl.semaphore_wait(barrier, len(peers))
 
     count = [0]
     sent = []
@@ -352,32 +364,32 @@
             wait(fb.at[it, o], fsem.at[4 * it + o])
         return ((fb[it, 0] + fb[it, 1]) + (fb[it, 2] + fb[it, 3])) + RIDGE * vector
 
-    planes = [(0, 2), (2, 1), (3, 1)]
-
-    def sum_start(k, values):
-        p, n = planes[k]
+    some = (TARGETS // 2, BLOCK)
+    match = lax.broadcasted_iota(jnp.int32, some, 0) == lax.broadcasted_iota(jnp.int32, some, 1)
+    sublane = lax.broadcasted_iota(jnp.int32, (8, BLOCK), 0)
+
+    def pack(values):
+        tile = jnp.zeros((8, BLOCK), F32)
         for i, value in enumerate(values):
-            xb[x, p + i] = value
-        for peer in xmates:
-            copy(xb.at[x, pl.ds(p, n)], xb.at[x, pl.ds(p, n)], xsem.at[4 * k + x], peer)
-
-    def sum_finish(k):
-        p, n = planes[k]
-        for o in xothers:
-            wait(xb.at[o, pl.ds(p, n)], xsem.at[4 * k + o])
-        for i in range(p, p + n):
-            db[b, i] = (xb[0, i] + xb[1, i]) + (xb[2, i] + xb[3, i])
-        for peer in bmates:
-            copy(db.at[b, pl.ds(p, n)], db.at[b, pl.ds(p, n)], dsem.at[8 * k + b], peer)
-        for o in bothers:
-            wait(db.at[o, pl.ds(p, n)], dsem.at[8 * k + o])
-        out = []
-        for i in range(p, p + n):
-            total = db[0, i]
-            for o in range(1, 8):
-                total = total + db[o, i]
-            out.append(jnp.sum(total, axis=1, keepdims=True))
-        return out
+            sums = jnp.where(match, jnp.sum(value, axis=1, keepdims=True), 0.0)
+            tile = jnp.where(sublane == i, jnp.sum(sums, axis=0, keepdims=True), tile)
+        return tile
+
+    def unpack(tile, i):
+        return jnp.sum(jnp.where(match, tile[i : i + 1], 0.0), axis=1, keepdims=True)
+
+    def share(base, mine, mates, tile):
+        sums[base + mine] = tile
+        for peer in mates:
+            copy(sums.at[base + mine], sums.at[base + mine], xsem.at[base + mine], peer)
+
+    def shared(base, others):
+        for o in others:
+            wait(sums.at[base + o], xsem.at[base + o])
+        total = sums[base]
+        for i in range(1, len(others) + 1):
+            total = total + sums[base + i]
+        return total
 
     multiply(0, True)
     r0 = first[...]
@@ -385,38 +397,31 @@
     w1buf[...] = w1
     place = lax.rem(b, 2) * 4 + x
     for peer in spread_to:
-        copy(w1buf, vj.at[1, :, lanes(place)], tsem.at[place], peer, peer[0] * 8 + peer[1] != s * 8 + j)
-
-    @pl.when(loop)
-    def _():
-        vj[1, :, lanes(place)] = w1
-
-    sum_start(0, [r0 * r0, r0 * w1])
-    for i, peer in enumerate(spread_from):
-
-        @pl.when(peer[0] * 8 + peer[1] != s * 8 + j)
-        def _(i=i):
-            wait(vj.at[1, :, BLOCK * i : BLOCK * (i + 1)], tsem.at[i])
-
+        copy(w1buf, vj.at[1, :, lanes(place)], tsem.at[place], peer)
+    share(0, x, xmates, pack([r0 * r0, r0 * w1, w1 * w1]))
+    share(4, b, bmates, shared(0, xothers))
+    for i in range(8):
+        wait(vj.at[1, :, BLOCK * i : BLOCK * (i + 1)], tsem.at[i])
     multiply(1, False)
-    rr0, curve0 = sum_finish(0)
+    tile = shared(4, bothers)
+    rr0, curve0, square = (unpack(tile, i) for i in range(3))
     a0 = rr0 / curve0
+    mu = square / curve0
     r1 = r0 - a0 * w1
-    sum_start(1, [r1 * r1])
-    (rr1,) = sum_finish(1)
-    b0 = rr1 / rr0
-    d1 = r1 + b0 * r0
-    w2 = image(1, w1)
-    image1 = (w1 - a0 * w2) + b0 * w1
-    sum_start(2, [d1 * image1])
-    (curve1,) = sum_finish(2)
-    a1 = rr1 / curve1
+    u = w1 - mu * r0
+    piece = fb[1, zl] - (0.25 * (mu - RIDGE)) * w1
+    share(12, x, xmates, pack([u * piece, 0.25 * (r1 * u)]))
+    share(16, y, ymates, shared(12, xothers))
+    share(20, z, rmates, shared(16, yothers))
+    image1 = image(1, w1) - mu * w1
+    tile = shared(20, rothers)
+    tau = unpack(tile, 1) / unpack(tile, 0)
     for core in (0, 1):
 
         @pl.when(c == core)
         def _(core=core):
-            fin[0, 32 * core : 32 * core + 32] = a0 * r0 + a1 * d1
-            fin[1, 32 * core : 32 * core + 32] = r1 - a1 * image1
+            fin[0, 32 * core : 32 * core + 32] = a0 * r0 + tau * u
+            fin[1, 32 * core : 32 * core + 32] = r1 - tau * image1
 
     copy(fin.at[:, half], fin.at[:, half], esem, sibling)
     wait(fin.at[:, other_half], esem)
@@ -435,7 +440,7 @@
     vector, some = (TARGETS, BLOCK), (TARGETS // 2, BLOCK)
     shapes = [
         (3, 2, BLOCK, WIDTH), (BLOCK, WIDTH), (BLOCK, WIDTH), (BLOCK, WIDTH), (8,) + vector, (TARGETS, WIDTH),
-        (2, TARGETS // 2, 2 * WIDTH), some, (2, 4) + some, (4, 4) + some, (8, 4) + some, some, (2,) + vector,
+        (2, TARGETS // 2, 2 * WIDTH), some, (2, 4) + some, (28, 8, BLOCK), some, (2,) + vector,
     ]
     return pl.pallas_call(
         solve_kernel,
@@ -448,8 +453,8 @@
         out_specs=(vmem,) * 3,
         scratch_shapes=[pltpu.VMEM(shape, F32) for shape in shapes]
         + [
-            dma((80,)), dma((8,)), dma((4,)), dma, dma, dma((6,)), dma, dma, dma((8,)), dma((8,)),
-            dma((12,)), dma((24,)), dma,
+            dma((96,)), dma((8,)), dma((4,)), dma, dma, dma((6,)), dma, dma, dma((8,)), dma((8,)),
+            dma((28,)), dma,
         ],
         compiler_params=pltpu.CompilerParams(collective_id=1, has_side_effects=True, vmem_limit_bytes=24 << 20),
         name="solve",

time: 146 us -> 128 us (0.88)
  Pallas kernels: 141 us -> 123 us
    pallas_call x1, Pallas kernels: 86 us -> 68.6 us  [solve(): pl.pallas_call(solve_kernel, out_shape=(jax.ShapeDtypeStruct(vector, F32)...]
where the time goes in v3:
time: 128 us
  Pallas kernels  123 us (96%)
  local copies, waits for them, and re-layouts  3.34 us (3%)
    pallas_call x1, Pallas kernels, solve(): pl.pallas_call(solve_kernel, out_shape=(jax.ShapeDtypeStruct(vector, F32)...  68.6 us
    pallas_call x1, Pallas kernels, gather(): pl.pallas_call(gather_kernel, out_shape=(jax.ShapeDtypeStruct((4, ROWS, D...  32.9 us
    pallas_call x1, Pallas kernels, build(): pl.pallas_call(build_kernel, out_shape=(jax.ShapeDtypeStruct((4, 2, BLOCK...  21.8 us
    unnamed x12, local copies, waits for them, and re-layouts  3.21 us

profile of v3, /device:TPU:1, one launch (start us, length us, event | category | flops | bytes accessed | tf_op | source)
XLA Modules:
  0.0 128.3 jit_solution(16588584481263859123)
XLA Ops:
  0.6 0.0 copy-start.2
  0.6 0.0 copy-start.1
  0.6 0.8 reduce
  1.4 0.1 broadcast_in_dim.8
  1.6 1.3 copy.7
  2.8 0.0 copy-start
  2.9 0.0 copy-start.3
  2.9 0.1 pad_maximum_fusion.frq
  2.9 0.0 copy-done.2
  2.9 0.0 copy-done.1
  3.0 32.9 %gather.1 = (bf16[4,1024,512]{2,1,0:T(8,128)(2,1)S(1)}, bf16[4,64,1024]{2,1,0:T(8,128)(2,1)S(1)}, bf16[1024,640]{1,0:T(8,128)(2,1)S(1)}) custom-call(bf16[1024,512]{1,0:T(8,128)(2,1)S(1)} %copy-done.1, bf16[64,1024]{1,0:T(8,128)(2,1)S(1)} %bitcast.6, bf16[512,640]{1,0:T(8,128)(2,1)S(1)} %pad_maximum_fusion.frq), custom_call_target="tpu_custom_call" | custom-call | tf_op jit(solution)/shard_map/gather/pallas_call | solution.py:153
  35.9 0.0 copy-done
  35.9 0.0 copy-done.3
  35.9 21.8 %build.1 = (f32[4,2,128,512]{3,2,1,0:T(8,128)S(1)}, f32[64,128]{1,0:T(8,128)S(1)}) custom-call(bf16[4096,512]{1,0:T(8,128)(2,1)S(1)} %bitcast.5, bf16[4,64,1024]{2,1,0:T(8,128)(2,1)S(1)} %get-tuple-element.12.tgt, bf16[1024,640]{1,0:T(8,128)(2,1)S(1)} %get-tuple-element.13.frow, bf16[512,512]{1,0:T(8,128)(2,1)S(1)} %copy-done, bf16[1,512]{1,0:T(2,128)(2,1)S(1)} %copy-done.3), custom_call_target="tpu_custom_call" | custom-call | tf_op jit(solution)/shard_map/build/pallas_call | solution.py:203
  57.7 68.6 %solve.1 = (f32[64,128]{1,0:T(8,128)S(1)}, f32[64,128]{1,0:T(8,128)S(1)}, f32[128,512]{1,0:T(8,128)S(1)}) custom-call(f32[4,2,128,512]{3,2,1,0:T(8,128)S(1)} %get-tuple-element.14.part, f32[64,128]{1,0:T(8,128)S(1)} %get-tuple-element.15.rhs), custom_call_target="tpu_custom_call" | custom-call | tf_op jit(solution)/shard_map/solve/pallas_call | solution.py:445
  126.4 0.6 copy.11
  127.0 0.6 copy.12
  127.6 0.7 copy.13
Async XLA Ops:
  0.6 2.3 %copy-start.2 = (bf16[1024,64]{0,1:T(8,128)(2,1)S(1)}, bf16[1024,64]{0,1:T(8,128)(2,1)}, u32[]{:S(2)}) copy-start(bf16[1024,64]{0,1:T(8,128)(2,1)} %param.7) | copy-start | bytes 393220
  0.6 2.3 %copy-start.1 = (bf16[1024,512]{1,0:T(8,128)(2,1)S(1)}, bf16[1024,512]{1,0:T(8,128)(2,1)}, u32[]{:S(2)}) copy-start(bf16[1024,512]{1,0:T(8,128)(2,1)} %cnt.1) | copy-start | bytes 3145732
  2.8 33.0 %copy-start = (bf16[512,512]{1,0:T(8,128)(2,1)S(1)}, bf16[512,512]{1,0:T(8,128)(2,1)}, u32[]{:S(2)}) copy-start(bf16[512,512]{1,0:T(8,128)(2,1)} %fcol.1) | copy-start | bytes 1572868
  2.9 33.0 %copy-start.3 = (bf16[1,512]{1,0:T(2,128)(2,1)S(1)}, bf16[1,512]{1,0:T(2,128)(2,1)}, u32[]{:S(2)}) copy-start(bf16[1,512]{1,0:T(2,128)(2,1)} %phase.1) | copy-start | bytes 3076

commit v4 on v3

--- a/solution.py
+++ b/solution.py
@@ -171,63 +171,9 @@
     )(counters, targets, frequencies)
 
 
-def build_kernel(cnt, tgt, frow, fcol, phase, part, rhs, zrow, gram, right):
-    step = pl.program_id(0)
-    j = lax.axis_index("feat")
-
-    @pl.when(step == 0)
-    def _():
-        gram[...] = jnp.zeros_like(gram)
-        right[...] = jnp.zeros_like(right)
-
-    nt = (((1,), (1,)), ((), ()))
-    rows = cnt[...]
-    zcol = cosine(jnp.dot(rows, fcol[...], preferred_element_type=F32) + phase[...].astype(F32))
-    mixed = lax.dot_general(frow[:, :DEPTH], rows, nt, preferred_element_type=F32)
-    zrow[...] = cosine(mixed + frow[:, DEPTH : DEPTH + 1].astype(F32))
-    gram[...] += jnp.dot(zrow[...], zcol, preferred_element_type=F32)
-    own = zrow[pl.ds(pl.multiple_of(BLOCK * j, BLOCK), BLOCK), :]
-    right[...] += lax.dot_general(tgt[0], own, nt, preferred_element_type=F32)
-
-    @pl.when(step == pl.num_programs(0) - 1)
-    def _():
-        for block in range(8):
-            part[block % 4, block // 4] = gram[block * BLOCK : (block + 1) * BLOCK, :]
-        rhs[...] = right[...]
-
-
-def build(counters, targets, frow, fcol, phases):
-    steps = 4 * ROWS // STEP
-    per = ROWS // STEP
-    whole = lambda shape: pl.BlockSpec(shape, lambda i: (0,) * len(shape))
-    return pl.pallas_call(
-        build_kernel,
-        out_shape=(
-            jax.ShapeDtypeStruct((4, 2, BLOCK, WIDTH), F32),
-            jax.ShapeDtypeStruct((TARGETS, BLOCK), F32),
-        ),
-        grid=(steps,),
-        in_specs=[
-            pl.BlockSpec((STEP, DEPTH), lambda i: (i, 0)),
-            pl.BlockSpec((1, TARGETS, STEP), lambda i: (i // per, 0, i % per)),
-            whole((8 * BLOCK, DEPTH + 128)),
-            whole((DEPTH, WIDTH)),
-            whole((1, WIDTH)),
-        ],
-        out_specs=(whole((4, 2, BLOCK, WIDTH)), whole((TARGETS, BLOCK))),
-        scratch_shapes=[
-            pltpu.VMEM((8 * BLOCK, STEP), jnp.bfloat16),
-            pltpu.VMEM((8 * BLOCK, WIDTH), F32),
-            pltpu.VMEM((TARGETS, BLOCK), F32),
-        ],
-        compiler_params=pltpu.CompilerParams(vmem_limit_bytes=40 << 20),
-        name="build",
-    )(counters.reshape(4 * ROWS, DEPTH), targets, frow, fcol, phases)
-
-
 def solve_kernel(
-    part, rhs, sol, res, gram,
-    ybuf, zsend, zrecv, gother, rh, rj, vj, first, fb, sums, w1buf, fin,
+    cnt, tgt, frow, fcol, phase, sol, res, gram,
+    zcol, right, pair, acc, part, ybuf, zsend, zrecv, gother, rh, rj, vj, first, fb, sums, w1buf, fin,
     ssem, hsem, rsem, osem, psem, ysem, zsem, gsem, fsem, tsem, xsem, esem,
 ):
     s, j = lax.axis_index("samp"), lax.axis_index("feat")
@@ -269,6 +215,23 @@
     peers = xmates + bmates + fmates + across + spread_from
     for peer in peers:
         pl.semaphore_signal(barrier, inc=1, device_id=peer, device_id_type=MESH)
+
+    nt = (((1,), (1,)), ((), ()))
+    right[...] = jnp.zeros_like(right)
+
+    def features(block, rows):
+        mixed = lax.dot_general(block[:, :DEPTH], rows, nt, preferred_element_type=F32)
+        return cosine(mixed + block[:, DEPTH : DEPTH + 1].astype(F32))
+
+    @pl.loop(0, 4 * ROWS // STEP)
+    def _(i):
+        chunk = pl.ds(pl.multiple_of(i * STEP, STEP), STEP)
+        rows = cnt[chunk, :]
+        zcol[chunk, :] = cosine(jnp.dot(rows, fcol[...], preferred_element_type=F32) + phase[...].astype(F32))
+        own = features(frow[pl.ds(pl.multiple_of(BLOCK * j, BLOCK), BLOCK), :], rows)
+        columns = pl.ds(pl.multiple_of(lax.rem(i, 2) * STEP, STEP), STEP)
+        right[...] += lax.dot_general(tgt[lax.div(i, 2), :, columns], own, nt, preferred_element_type=F32)
+
     pl.semaphore_wait(barrier, len(peers))
 
     count = [0]
@@ -291,16 +254,27 @@
 
     half, other_half = pl.ds(32 * c, 32), pl.ds(32 * (1 - c), 32)
 
-    rh[b] = rhs[...]
+    rh[b] = right[...]
     for o, peer in zip(bothers, bmates):
         copy(rh.at[b], rh.at[b], hsem.at[b], peer)
-    for d in (1, 2, 3):
-        to = lax.rem(y + d, 4)
-        copy(part.at[to, 1 - zh], ybuf.at[d - 1, 0], ysem.at[d - 1], ((zh * 4 + to) * 4 + x, j))
-    for d in (1, 2, 3):
-        to = lax.rem(y + d, 4)
-        copy(part.at[to, zh], ybuf.at[d - 1, 1], ysem.at[d + 2], ((zh * 4 + to) * 4 + x, j))
-
+    def two_blocks(which, slot, first_d):
+        steps = (first_d, first_d + 1)
+        for n, d in enumerate(steps):
+            row = pl.multiple_of((which * 4 + lax.rem(y + d, 4)) * BLOCK, BLOCK)
+            pair[n * BLOCK : (n + 1) * BLOCK, :] = frow[pl.ds(row, BLOCK), :]
+        acc[...] = jnp.zeros_like(acc)
+
+        @pl.loop(0, 4 * ROWS // STEP)
+        def _(i):
+            chunk = pl.ds(pl.multiple_of(i * STEP, STEP), STEP)
+            acc[...] += jnp.dot(features(pair[...], cnt[chunk, :]), zcol[chunk, :], preferred_element_type=F32)
+
+        for n, d in enumerate(steps):
+            part[slot, d - 1] = acc[n * BLOCK : (n + 1) * BLOCK, :]
+            if d < 4:
+                copy(part.at[slot, d - 1], ybuf.at[d - 1, slot], ysem.at[3 * slot + d - 1], ymates[d - 1])
+
+    two_blocks(1 - zh, 0, 1)
     for o in bothers:
         wait(rh.at[o], hsem.at[o])
     total = rh[0]
@@ -318,6 +292,7 @@
 
     for o, peer in zip(fothers, fmates):
         copy(rj.at[pl.ds(32 * lax.rem(o, 2), 32), lanes(x)], first, psem, peer, diag)
+    two_blocks(1 - zh, 0, 3)
     for o in xothers:
         wait(rj.at[:, lanes(o)], rsem.at[o])
     for core in (0, 1):
@@ -327,17 +302,19 @@
             vj[0, :, core * WIDTH : (core + 1) * WIDTH] = rj[32 * core : 32 * core + 32, :]
 
     copy(rj.at[other_half, :], vj.at[0, :, lanes(c, WIDTH)], osem, sibling)
-
-    def over_y(which, slot):
-        total = part[y, which]
+    two_blocks(zh, 1, 1)
+    two_blocks(zh, 1, 3)
+
+    def over_y(slot):
+        total = part[slot, 3]
         for d in range(3):
             wait(ybuf.at[d, slot], ysem.at[3 * slot + d])
             total = total + ybuf[d, slot]
         return total
 
-    zsend[...] = over_y(1 - zh, 0)
+    zsend[...] = over_y(0)
     copy(zsend, zrecv, zsem, (((1 - zh) * 4 + y) * 4 + x, j))
-    gram[...] = over_y(zh, 1)
+    gram[...] = over_y(1)
     wait(vj.at[0, :, lanes(1 - c, WIDTH)], osem)
 
     @pl.when(jnp.logical_not(diag))
@@ -349,7 +326,6 @@
     copy(gram, gother, gsem, sibling)
 
     def multiply(it, wait_gram):
-        nt = (((1,), (1,)), ((), ()))
         own = lax.dot_general(vj[it, :, lanes(c, WIDTH)], gram[...], nt, precision=HIGHEST, preferred_element_type=F32)
         if wait_gram:
             wait(gother, gsem)
@@ -434,12 +410,12 @@
             pl.when(when)(made.wait_send)
 
 
-def solve(part, rhs):
+def solve(counters, targets, frow, fcol, phases):
     vmem = pl.BlockSpec(memory_space=pltpu.VMEM)
     dma = pltpu.SemaphoreType.DMA
     vector, some = (TARGETS, BLOCK), (TARGETS // 2, BLOCK)
     shapes = [
-        (3, 2, BLOCK, WIDTH), (BLOCK, WIDTH), (BLOCK, WIDTH), (BLOCK, WIDTH), (8,) + vector, (TARGETS, WIDTH),
+        (2, 4, BLOCK, WIDTH), (3, 2, BLOCK, WIDTH), (BLOCK, WIDTH), (BLOCK, WIDTH), (BLOCK, WIDTH), (8,) + vector, (TARGETS, WIDTH),
         (2, TARGETS // 2, 2 * WIDTH), some, (2, 4) + some, (28, 8, BLOCK), some, (2,) + vector,
     ]
     return pl.pallas_call(
@@ -449,23 +425,28 @@
             jax.ShapeDtypeStruct(vector, F32),
             jax.ShapeDtypeStruct((BLOCK, WIDTH), F32),
         ),
-        in_specs=[vmem] * 2,
+        in_specs=[vmem] * 5,
         out_specs=(vmem,) * 3,
-        scratch_shapes=[pltpu.VMEM(shape, F32) for shape in shapes]
+        scratch_shapes=[
+            pltpu.VMEM((4 * ROWS, WIDTH), jnp.bfloat16),
+            pltpu.VMEM(vector, F32),
+            pltpu.VMEM((2 * BLOCK, DEPTH + 128), jnp.bfloat16),
+            pltpu.VMEM((2 * BLOCK, WIDTH), F32),
+        ]
+        + [pltpu.VMEM(shape, F32) for shape in shapes]
         + [
             dma((96,)), dma((8,)), dma((4,)), dma, dma, dma((6,)), dma, dma, dma((8,)), dma((8,)),
             dma((28,)), dma,
         ],
-        compiler_params=pltpu.CompilerParams(collective_id=1, has_side_effects=True, vmem_limit_bytes=24 << 20),
+        compiler_params=pltpu.CompilerParams(collective_id=1, has_side_effects=True, vmem_limit_bytes=40 << 20),
         name="solve",
-    )(part, rhs)
+    )(counters.reshape(4 * ROWS, DEPTH), targets, frow, fcol, phases)
 
 
 def on_device(counters, frequencies, phases, targets):
     columns = jnp.concatenate([frequencies.T, jnp.broadcast_to(phases.T, (WIDTH, 128))], axis=1)
     all_counters, all_targets, rows = gather(counters, targets.T, columns)
-    part, rhs = build(all_counters, all_targets, rows, frequencies, phases)
-    solution, residual, gram = solve(part, rhs)
+    solution, residual, gram = solve(all_counters, all_targets, rows, frequencies, phases)
     return solution.T, residual.T, gram
 
 

time: 128 us -> 123 us (0.961)
  Pallas kernels: 123 us -> 118 us
    pallas_call x1 -> x0, Pallas kernels: 21.8 us -> none  [build(): pl.pallas_call(build_kernel, out_shape=(jax.ShapeDtypeStruct((4, 2, BLOCK...]
    pallas_call x1, Pallas kernels: 68.6 us -> 84.9 us  [solve(): pl.pallas_call(solve_kernel, out_shape=(jax.ShapeDtypeStruct(vector, F32)...]
where the time goes in v4:
time: 123 us
  Pallas kernels  118 us (96%)
  local copies, waits for them, and re-layouts  3.34 us (3%)
    pallas_call x1, Pallas kernels, solve(): pl.pallas_call(solve_kernel, out_shape=(jax.ShapeDtypeStruct(vector, F32)...  84.9 us
    pallas_call x1, Pallas kernels, gather(): pl.pallas_call(gather_kernel, out_shape=(jax.ShapeDtypeStruct((4, ROWS, D...  32.9 us
    unnamed x12, local copies, waits for them, and re-layouts  3.21 us

profile of v4, /device:TPU:1, one launch (start us, length us, event | category | flops | bytes accessed | tf_op | source)
XLA Modules:
  0.0 122.8 jit_solution(558521968851381903)
XLA Ops:
  0.6 0.0 copy-start.2
  0.6 0.0 copy-start.1
  0.6 0.8 reduce
  1.4 0.1 broadcast_in_dim.8
  1.6 1.3 %copy.7 = bf16[512,512]{0,1:T(8,128)(2,1)S(1)} copy(bf16[512,512]{1,0:T(8,128)(2,1)} %fcol.1) | data formatting | bytes 1048576 | tf_op args[1]
  2.8 0.0 copy-start
  2.9 0.0 copy-start.3
  2.9 0.1 pad_maximum_fusion.frq
  2.9 0.0 copy-done.2
  2.9 0.0 copy-done.1
  3.0 32.9 %gather.1 = (bf16[4,1024,512]{2,1,0:T(8,128)(2,1)S(1)}, bf16[4,64,1024]{2,1,0:T(8,128)(2,1)S(1)}, bf16[1024,640]{1,0:T(8,128)(2,1)S(1)}) custom-call(bf16[1024,512]{1,0:T(8,128)(2,1)S(1)} %copy-done.1, bf16[64,1024]{1,0:T(8,128)(2,1)S(1)} %bitcast.6, bf16[512,640]{1,0:T(8,128)(2,1)S(1)} %pad_maximum_fusion.frq), custom_call_target="tpu_custom_call" | custom-call | tf_op jit(solution)/shard_map/gather/pallas_call | solution.py:153
  35.9 0.0 copy-done
  35.9 0.0 copy-done.3
  35.9 84.9 %solve.1 = (f32[64,128]{1,0:T(8,128)S(1)}, f32[64,128]{1,0:T(8,128)S(1)}, f32[128,512]{1,0:T(8,128)S(1)}) custom-call(bf16[4096,512]{1,0:T(8,128)(2,1)S(1)} %bitcast.5, bf16[4,64,1024]{2,1,0:T(8,128)(2,1)S(1)} %get-tuple-element.10.tgt, bf16[1024,640]{1,0:T(8,128)(2,1)S(1)} %get-tuple-element.11.frow, bf16[512,512]{1,0:T(8,128)(2,1)S(1)} %copy-done, ...), custom_call_target="tpu_custom_call" | custom-call | tf_op jit(solution)/shard_map/solve/pallas_call | solution.py:421
  120.8 0.6 copy.11
  121.5 0.6 copy.12
  122.1 0.7 copy.13
Async XLA Ops:
  0.6 2.3 %copy-start.2 = (bf16[1024,64]{0,1:T(8,128)(2,1)S(1)}, bf16[1024,64]{0,1:T(8,128)(2,1)}, u32[]{:S(2)}) copy-start(bf16[1024,64]{0,1:T(8,128)(2,1)} %param.7) | copy-start | bytes 393220
  0.6 2.3 %copy-start.1 = (bf16[1024,512]{1,0:T(8,128)(2,1)S(1)}, bf16[1024,512]{1,0:T(8,128)(2,1)}, u32[]{:S(2)}) copy-start(bf16[1024,512]{1,0:T(8,128)(2,1)} %cnt.1) | copy-start | bytes 3145732
  2.8 33.0 %copy-start = (bf16[512,512]{1,0:T(8,128)(2,1)S(1)}, bf16[512,512]{1,0:T(8,128)(2,1)}, u32[]{:S(2)}) copy-start(bf16[512,512]{1,0:T(8,128)(2,1)} %fcol.1) | copy-start | bytes 1572868
  2.9 33.0 %copy-start.3 = (bf16[1,512]{1,0:T(2,128)(2,1)S(1)}, bf16[1,512]{1,0:T(2,128)(2,1)}, u32[]{:S(2)}) copy-start(bf16[1,512]{1,0:T(2,128)(2,1)} %phase.1) | copy-start | bytes 3076

commit v5 on v4

--- a/solution.py
+++ b/solution.py
@@ -41,7 +41,7 @@
     pl.semaphore_wait(barrier, len(peers))
 
 
-def gather_kernel(cnt, tgt, frq, cg, tg, fr, ssem, rsem, fsend, frecv, lsem):
+def gather_kernel(cnt, tgt, frq, fcol, phase, cg, tg, fr, zcol, ssem, rsem, fsend, frecv, lsem):
     s, j = lax.axis_index("samp"), lax.axis_index("feat")
     x, c, zl, zh = lax.rem(s, 4), lax.rem(j, 2), lax.div(j, 2), lax.div(s, 16)
     z = zh * 4 + zl
@@ -116,29 +116,43 @@
         pltpu.make_async_copy(frq.at[quarter], fr.at[mine], lsem.at[2]),
     ]
     go(local)
+    def columns(slot, rows):
+        mixed = jnp.dot(cg[slot, rows, :], fcol[...], preferred_element_type=F32)
+        zcol[slot, rows, :] = cosine(mixed + phase[...].astype(F32))
+
+    here, there = pl.ds(pl.multiple_of(half, STEP), STEP), pl.ds(pl.multiple_of(STEP - half, STEP), STEP)
+    local[0].wait()
+    columns(0, here)
     got(to_right[0])
     go(on_right)
     go(across[1, 0])
     got(to_left[1])
     go(on_left)
     go(across[2, 1])
+    columns(0, there)
     got(to_right[1])
     go(across[1, 1])
     got(to_left[0])
     go(across[2, 0])
+    columns(1, here)
+    columns(2, here)
     got(on_right)
     go(across[3, 0])
     got(on_left)
     go(across[3, 1])
-    for (slot, part), copies in across.items():
-        got(twin(6 + 2 * (slot - 1) + part, slot, part))
+    for slot in (1, 2, 3):
+        if slot == 3:
+            columns(3, here)
+        for part in (0, 1):
+            got(twin(6 + 2 * (slot - 1) + part, slot, part))
+        columns(slot, there)
     for i, (dz, core) in enumerate([(-1, 0), (-1, 1), (1, 0), (1, 1), (-2, 0), (2, 1)]):
         source = along_z(dz, core)
         rows = pl.ds(pl.multiple_of(BLOCK * source[1], BLOCK), BLOCK)
         remote(frq.at[quarter], fr.at[rows], fsend.at[i], frecv.at[2 * (i // 2) + core], source).wait_recv()
     rows = pl.ds(pl.multiple_of(BLOCK * sibling[1], BLOCK), BLOCK)
     remote(frq.at[quarter], fr.at[rows], fsend.at[6], frecv.at[6], sibling).wait_recv()
-    for copy in local:
+    for copy in local[1:]:
         copy.wait()
     sent = to_right[0] + to_right[1] + to_left[0] + to_left[1] + on_right + on_left + spread
     for copies in across.values():
@@ -147,18 +161,19 @@
         copy.wait_send()
 
 
-def gather(counters, targets, frequencies):
+def gather(counters, targets, frequencies, columns, phases):
     bf16 = jnp.bfloat16
-    hbm = pl.BlockSpec(memory_space=pl.ANY)
+    vmem = pl.BlockSpec(memory_space=pltpu.VMEM)
     return pl.pallas_call(
         gather_kernel,
         out_shape=(
             jax.ShapeDtypeStruct((4, ROWS, DEPTH), bf16),
             jax.ShapeDtypeStruct((4, TARGETS, ROWS), bf16),
             jax.ShapeDtypeStruct((8 * BLOCK, DEPTH + 128), bf16),
+            jax.ShapeDtypeStruct((4, ROWS, WIDTH), bf16),
         ),
-        in_specs=[hbm] * 3,
-        out_specs=(hbm,) * 3,
+        in_specs=[vmem] * 5,
+        out_specs=(vmem,) * 4,
         scratch_shapes=[
             pltpu.SemaphoreType.DMA((24,)),
             pltpu.SemaphoreType.DMA((24,)),
@@ -166,14 +181,14 @@
             pltpu.SemaphoreType.DMA((7,)),
             pltpu.SemaphoreType.DMA((3,)),
         ],
-        compiler_params=pltpu.CompilerParams(collective_id=0, has_side_effects=True, vmem_limit_bytes=4 << 20),
+        compiler_params=pltpu.CompilerParams(collective_id=0, has_side_effects=True, vmem_limit_bytes=32 << 20),
         name="gather",
-    )(counters, targets, frequencies)
+    )(counters, targets, frequencies, columns, phases)
 
 
 def solve_kernel(
-    cnt, tgt, frow, fcol, phase, sol, res, gram,
-    zcol, right, pair, acc, part, ybuf, zsend, zrecv, gother, rh, rj, vj, first, fb, sums, w1buf, fin,
+    cnt, tgt, frow, zcol, sol, res, gram,
+    right, pair, acc, part, ybuf, zsend, zrecv, gother, rh, rj, vj, first, fb, sums, w1buf, fin,
     ssem, hsem, rsem, osem, psem, ysem, zsem, gsem, fsem, tsem, xsem, esem,
 ):
     s, j = lax.axis_index("samp"), lax.axis_index("feat")
@@ -216,24 +231,6 @@
     for peer in peers:
         pl.semaphore_signal(barrier, inc=1, device_id=peer, device_id_type=MESH)
 
-    nt = (((1,), (1,)), ((), ()))
-    right[...] = jnp.zeros_like(right)
-
-    def features(block, rows):
-        mixed = lax.dot_general(block[:, :DEPTH], rows, nt, preferred_element_type=F32)
-        return cosine(mixed + block[:, DEPTH : DEPTH + 1].astype(F32))
-
-    @pl.loop(0, 4 * ROWS // STEP)
-    def _(i):
-        chunk = pl.ds(pl.multiple_of(i * STEP, STEP), STEP)
-        rows = cnt[chunk, :]
-        zcol[chunk, :] = cosine(jnp.dot(rows, fcol[...], preferred_element_type=F32) + phase[...].astype(F32))
-        own = features(frow[pl.ds(pl.multiple_of(BLOCK * j, BLOCK), BLOCK), :], rows)
-        columns = pl.ds(pl.multiple_of(lax.rem(i, 2) * STEP, STEP), STEP)
-        right[...] += lax.dot_general(tgt[lax.div(i, 2), :, columns], own, nt, preferred_element_type=F32)
-
-    pl.semaphore_wait(barrier, len(peers))
-
     count = [0]
     sent = []
 
@@ -254,9 +251,12 @@
 
     half, other_half = pl.ds(32 * c, 32), pl.ds(32 * (1 - c), 32)
 
-    rh[b] = right[...]
-    for o, peer in zip(bothers, bmates):
-        copy(rh.at[b], rh.at[b], hsem.at[b], peer)
+    nt = (((1,), (1,)), ((), ()))
+
+    def features(block, rows):
+        mixed = lax.dot_general(block[:, :DEPTH], rows, nt, preferred_element_type=F32)
+        return cosine(mixed + block[:, DEPTH : DEPTH + 1].astype(F32))
+
     def two_blocks(which, slot, first_d):
         steps = (first_d, first_d + 1)
         for n, d in enumerate(steps):
@@ -269,12 +269,29 @@
             chunk = pl.ds(pl.multiple_of(i * STEP, STEP), STEP)
             acc[...] += jnp.dot(features(pair[...], cnt[chunk, :]), zcol[chunk, :], preferred_element_type=F32)
 
+        if (slot, first_d) == (0, 1):
+            pl.semaphore_wait(barrier, len(peers))
         for n, d in enumerate(steps):
             part[slot, d - 1] = acc[n * BLOCK : (n + 1) * BLOCK, :]
             if d < 4:
                 copy(part.at[slot, d - 1], ybuf.at[d - 1, slot], ysem.at[3 * slot + d - 1], ymates[d - 1])
 
     two_blocks(1 - zh, 0, 1)
+    right[...] = jnp.zeros_like(right)
+
+    @pl.loop(0, 4 * ROWS // STEP)
+    def _(i):
+        own = features(
+            frow[pl.ds(pl.multiple_of(BLOCK * j, BLOCK), BLOCK), :],
+            cnt[pl.ds(pl.multiple_of(i * STEP, STEP), STEP), :],
+        )
+        columns = pl.ds(pl.multiple_of(lax.rem(i, 2) * STEP, STEP), STEP)
+        right[...] += lax.dot_general(tgt[lax.div(i, 2), :, columns], own, nt, preferred_element_type=F32)
+
+    rh[b] = right[...]
+    for o, peer in zip(bothers, bmates):
+        copy(rh.at[b], rh.at[b], hsem.at[b], peer)
+    two_blocks(1 - zh, 0, 3)
     for o in bothers:
         wait(rh.at[o], hsem.at[o])
     total = rh[0]
@@ -292,18 +309,7 @@
 
     for o, peer in zip(fothers, fmates):
         copy(rj.at[pl.ds(32 * lax.rem(o, 2), 32), lanes(x)], first, psem, peer, diag)
-    two_blocks(1 - zh, 0, 3)
-    for o in xothers:
-        wait(rj.at[:, lanes(o)], rsem.at[o])
-    for core in (0, 1):
-
-        @pl.when(c == core)
-        def _(core=core):
-            vj[0, :, core * WIDTH : (core + 1) * WIDTH] = rj[32 * core : 32 * core + 32, :]
-
-    copy(rj.at[other_half, :], vj.at[0, :, lanes(c, WIDTH)], osem, sibling)
     two_blocks(zh, 1, 1)
-    two_blocks(zh, 1, 3)
 
     def over_y(slot):
         total = part[slot, 3]
@@ -314,6 +320,16 @@
 
     zsend[...] = over_y(0)
     copy(zsend, zrecv, zsem, (((1 - zh) * 4 + y) * 4 + x, j))
+    two_blocks(zh, 1, 3)
+    for o in xothers:
+        wait(rj.at[:, lanes(o)], rsem.at[o])
+    for core in (0, 1):
+
+        @pl.when(c == core)
+        def _(core=core):
+            vj[0, :, core * WIDTH : (core + 1) * WIDTH] = rj[32 * core : 32 * core + 32, :]
+
+    copy(rj.at[other_half, :], vj.at[0, :, lanes(c, WIDTH)], osem, sibling)
     gram[...] = over_y(1)
     wait(vj.at[0, :, lanes(1 - c, WIDTH)], osem)
 
@@ -410,7 +426,7 @@
             pl.when(when)(made.wait_send)
 
 
-def solve(counters, targets, frow, fcol, phases):
+def solve(counters, targets, frow, zcol):
     vmem = pl.BlockSpec(memory_space=pltpu.VMEM)
     dma = pltpu.SemaphoreType.DMA
     vector, some = (TARGETS, BLOCK), (TARGETS // 2, BLOCK)
@@ -425,10 +441,9 @@
             jax.ShapeDtypeStruct(vector, F32),
             jax.ShapeDtypeStruct((BLOCK, WIDTH), F32),
         ),
-        in_specs=[vmem] * 5,
+        in_specs=[vmem] * 4,
         out_specs=(vmem,) * 3,
         scratch_shapes=[
-            pltpu.VMEM((4 * ROWS, WIDTH), jnp.bfloat16),
             pltpu.VMEM(vector, F32),
             pltpu.VMEM((2 * BLOCK, DEPTH + 128), jnp.bfloat16),
             pltpu.VMEM((2 * BLOCK, WIDTH), F32),
@@ -440,13 +455,12 @@
         ],
         compiler_params=pltpu.CompilerParams(collective_id=1, has_side_effects=True, vmem_limit_bytes=40 << 20),
         name="solve",
-    )(counters.reshape(4 * ROWS, DEPTH), targets, frow, fcol, phases)
+    )(counters.reshape(4 * ROWS, DEPTH), targets, frow, zcol.reshape(4 * ROWS, WIDTH))
 
 
 def on_device(counters, frequencies, phases, targets):
     columns = jnp.concatenate([frequencies.T, jnp.broadcast_to(phases.T, (WIDTH, 128))], axis=1)
-    all_counters, all_targets, rows = gather(counters, targets.T, columns)
-    solution, residual, gram = solve(all_counters, all_targets, rows, frequencies, phases)
+    solution, residual, gram = solve(*gather(counters, targets.T, columns, frequencies, phases))
     return solution.T, residual.T, gram
 
 

time: 123 us -> 115 us (0.935)
  Pallas kernels: 118 us -> 110 us
    pallas_call x1, Pallas kernels: 84.9 us -> 75.9 us  [solve(): pl.pallas_call(solve_kernel, out_shape=(jax.ShapeDtypeStruct(vector, F32)...]
where the time goes in v5:
time: 115 us
  Pallas kernels  110 us (96%)
  local copies, waits for them, and re-layouts  3.34 us (3%)
    pallas_call x1, Pallas kernels, solve(): pl.pallas_call(solve_kernel, out_shape=(jax.ShapeDtypeStruct(vector, F32)...  75.9 us
    pallas_call x1, Pallas kernels, gather(): pl.pallas_call(gather_kernel, out_shape=(jax.ShapeDtypeStruct((4, ROWS, D...  33.8 us
    unnamed x12, local copies, waits for them, and re-layouts  3.21 us

profile of v5, /device:TPU:1, one launch (start us, length us, event | category | flops | bytes accessed | tf_op | source)
XLA Modules:
  0.0 114.7 jit_solution(3319637967056572130)
XLA Ops:
  0.6 0.0 copy-start.3
  0.6 0.0 copy-start
  0.7 0.0 copy-start.2
  0.7 0.0 copy-start.1
  0.7 0.8 reduce
  1.5 0.1 broadcast_in_dim.8
  1.6 1.3 %copy.7 = bf16[512,512]{0,1:T(8,128)(2,1)S(1)} copy(bf16[512,512]{1,0:T(8,128)(2,1)} %fcol.1) | data formatting | bytes 1048576 | tf_op args[1]
  2.9 0.1 pad_maximum_fusion.frq
  3.0 0.0 copy-done.3
  3.0 0.0 copy-done
  3.0 0.0 copy-done.2
  3.0 0.0 copy-done.1
  3.0 33.8 %gather.1 = (bf16[4,1024,512]{2,1,0:T(8,128)(2,1)S(1)}, bf16[4,64,1024]{2,1,0:T(8,128)(2,1)S(1)}, bf16[1024,640]{1,0:T(8,128)(2,1)S(1)}, bf16[4,1024,512]{2,1,0:T(8,128)(2,1)S(1)}) custom-call(bf16[1024,512]{1,0:T(8,128)(2,1)S(1)} %copy-done.1, bf16[64,1024]{1,0:T(8,128)(2,1)S(1)} %bitcast.8, bf16[512,640]{1,0:T(8,128)(2,1)S(1)} %pad_maximum_fusion.frq, ...), custom_call_target="tpu_custom_call" | custom-call | tf_op jit(solution)/shard_map/gather/pallas_call | solution.py:167
  36.8 75.9 %solve.1 = (f32[64,128]{1,0:T(8,128)S(1)}, f32[64,128]{1,0:T(8,128)S(1)}, f32[128,512]{1,0:T(8,128)S(1)}) custom-call(bf16[4096,512]{1,0:T(8,128)(2,1)S(1)} %bitcast.6, bf16[4,64,1024]{2,1,0:T(8,128)(2,1)S(1)} %get-tuple-element.11.tgt, bf16[1024,640]{1,0:T(8,128)(2,1)S(1)} %get-tuple-element.12.frow, bf16[4096,512]{1,0:T(8,128)(2,1)S(1)} %bitcast.7), custom_call_target="tpu_custom_call" | custom-call | tf_op jit(solution)/shard_map/solve/pallas_call | solution.py:437
  112.7 0.6 copy.11
  113.3 0.6 copy.12
  114.0 0.7 copy.13
Async XLA Ops:
  0.6 2.3 %copy-start.3 = (bf16[1,512]{1,0:T(2,128)(2,1)S(1)}, bf16[1,512]{1,0:T(2,128)(2,1)}, u32[]{:S(2)}) copy-start(bf16[1,512]{1,0:T(2,128)(2,1)} %phase.1) | copy-start | bytes 3076
  0.6 2.3 %copy-start = (bf16[512,512]{1,0:T(8,128)(2,1)S(1)}, bf16[512,512]{1,0:T(8,128)(2,1)}, u32[]{:S(2)}) copy-start(bf16[512,512]{1,0:T(8,128)(2,1)} %fcol.1) | copy-start | bytes 1572868
  0.7 2.3 %copy-start.2 = (bf16[1024,64]{0,1:T(8,128)(2,1)S(1)}, bf16[1024,64]{0,1:T(8,128)(2,1)}, u32[]{:S(2)}) copy-start(bf16[1024,64]{0,1:T(8,128)(2,1)} %param.7) | copy-start | bytes 393220
  0.7 2.3 %copy-start.1 = (bf16[1024,512]{1,0:T(8,128)(2,1)S(1)}, bf16[1024,512]{1,0:T(8,128)(2,1)}, u32[]{:S(2)}) copy-start(bf16[1024,512]{1,0:T(8,128)(2,1)} %cnt.1) | copy-start | bytes 3145732

commit v6 on v5

--- a/solution.py
+++ b/solution.py
@@ -28,6 +28,14 @@
     return (1.0 - root * root).astype(jnp.bfloat16)
 
 
+NT = (((1,), (1,)), ((), ()))
+
+
+def features(block, rows):
+    mixed = lax.dot_general(block[:, :DEPTH], rows, NT, preferred_element_type=F32)
+    return cosine(mixed + block[:, DEPTH : DEPTH + 1].astype(F32))
+
+
 def remote(src, dst, send_sem, recv_sem, device):
     return pltpu.make_async_remote_copy(
         src_ref=src, dst_ref=dst, send_sem=send_sem, recv_sem=recv_sem, device_id=device, device_id_type=MESH
@@ -41,7 +49,7 @@
     pl.semaphore_wait(barrier, len(peers))
 
 
-def gather_kernel(cnt, tgt, frq, fcol, phase, cg, tg, fr, zcol, ssem, rsem, fsend, frecv, lsem):
+def gather_kernel(cnt, tgt, frq, fcol, phase, cg, tg, fr, zcol, rpart, ssem, rsem, fsend, frecv, lsem):
     s, j = lax.axis_index("samp"), lax.axis_index("feat")
     x, c, zl, zh = lax.rem(s, 4), lax.rem(j, 2), lax.div(j, 2), lax.div(s, 16)
     z = zh * 4 + zl
@@ -119,9 +127,14 @@
     def columns(slot, rows):
         mixed = jnp.dot(cg[slot, rows, :], fcol[...], preferred_element_type=F32)
         zcol[slot, rows, :] = cosine(mixed + phase[...].astype(F32))
+        samples = pl.ds(pl.multiple_of(rows.start, STEP), STEP)
+        own = features(frq[quarter, :], cg[slot, rows, :])
+        rpart[...] += lax.dot_general(tg[slot, :, samples], own, NT, preferred_element_type=F32)
 
     here, there = pl.ds(pl.multiple_of(half, STEP), STEP), pl.ds(pl.multiple_of(STEP - half, STEP), STEP)
+    rpart[...] = jnp.zeros_like(rpart)
     local[0].wait()
+    local[1].wait()
     columns(0, here)
     got(to_right[0])
     go(on_right)
@@ -152,8 +165,7 @@
         remote(frq.at[quarter], fr.at[rows], fsend.at[i], frecv.at[2 * (i // 2) + core], source).wait_recv()
     rows = pl.ds(pl.multiple_of(BLOCK * sibling[1], BLOCK), BLOCK)
     remote(frq.at[quarter], fr.at[rows], fsend.at[6], frecv.at[6], sibling).wait_recv()
-    for copy in local[1:]:
-        copy.wait()
+    local[2].wait()
     sent = to_right[0] + to_right[1] + to_left[0] + to_left[1] + on_right + on_left + spread
     for copies in across.values():
         sent = sent + copies
@@ -171,9 +183,10 @@
             jax.ShapeDtypeStruct((4, TARGETS, ROWS), bf16),
             jax.ShapeDtypeStruct((8 * BLOCK, DEPTH + 128), bf16),
             jax.ShapeDtypeStruct((4, ROWS, WIDTH), bf16),
+            jax.ShapeDtypeStruct((TARGETS, BLOCK), F32),
         ),
         in_specs=[vmem] * 5,
-        out_specs=(vmem,) * 4,
+        out_specs=(vmem,) * 5,
         scratch_shapes=[
             pltpu.SemaphoreType.DMA((24,)),
             pltpu.SemaphoreType.DMA((24,)),
@@ -187,8 +200,8 @@
 
 
 def solve_kernel(
-    cnt, tgt, frow, zcol, sol, res, gram,
-    right, pair, acc, part, ybuf, zsend, zrecv, gother, rh, rj, vj, first, fb, sums, w1buf, fin,
+    cnt, frow, zcol, right, sol, res, gram,
+    pair, acc, part, ybuf, zsend, zrecv, gother, rh, rj, vj, first, fb, sums, w1buf, fin,
     ssem, hsem, rsem, osem, psem, ysem, zsem, gsem, fsem, tsem, xsem, esem,
 ):
     s, j = lax.axis_index("samp"), lax.axis_index("feat")
@@ -251,12 +264,6 @@
 
     half, other_half = pl.ds(32 * c, 32), pl.ds(32 * (1 - c), 32)
 
-    nt = (((1,), (1,)), ((), ()))
-
-    def features(block, rows):
-        mixed = lax.dot_general(block[:, :DEPTH], rows, nt, preferred_element_type=F32)
-        return cosine(mixed + block[:, DEPTH : DEPTH + 1].astype(F32))
-
     def two_blocks(which, slot, first_d):
         steps = (first_d, first_d + 1)
         for n, d in enumerate(steps):
@@ -271,27 +278,17 @@
 
         if (slot, first_d) == (0, 1):
             pl.semaphore_wait(barrier, len(peers))
+            for peer in bmates:
+                copy(right, rh.at[b], hsem.at[b], peer)
         for n, d in enumerate(steps):
             part[slot, d - 1] = acc[n * BLOCK : (n + 1) * BLOCK, :]
             if d < 4:
                 copy(part.at[slot, d - 1], ybuf.at[d - 1, slot], ysem.at[3 * slot + d - 1], ymates[d - 1])
 
     two_blocks(1 - zh, 0, 1)
-    right[...] = jnp.zeros_like(right)
-
-    @pl.loop(0, 4 * ROWS // STEP)
-    def _(i):
-        own = features(
-            frow[pl.ds(pl.multiple_of(BLOCK * j, BLOCK), BLOCK), :],
-            cnt[pl.ds(pl.multiple_of(i * STEP, STEP), STEP), :],
-        )
-        columns = pl.ds(pl.multiple_of(lax.rem(i, 2) * STEP, STEP), STEP)
-        right[...] += lax.dot_general(tgt[lax.div(i, 2), :, columns], own, nt, preferred_element_type=F32)
-
+    two_blocks(1 - zh, 0, 3)
+    two_blocks(zh, 1, 1)
     rh[b] = right[...]
-    for o, peer in zip(bothers, bmates):
-        copy(rh.at[b], rh.at[b], hsem.at[b], peer)
-    two_blocks(1 - zh, 0, 3)
     for o in bothers:
         wait(rh.at[o], hsem.at[o])
     total = rh[0]
@@ -309,7 +306,6 @@
 
     for o, peer in zip(fothers, fmates):
         copy(rj.at[pl.ds(32 * lax.rem(o, 2), 32), lanes(x)], first, psem, peer, diag)
-    two_blocks(zh, 1, 1)
 
     def over_y(slot):
         total = part[slot, 3]
@@ -342,11 +338,11 @@
     copy(gram, gother, gsem, sibling)
 
     def multiply(it, wait_gram):
-        own = lax.dot_general(vj[it, :, lanes(c, WIDTH)], gram[...], nt, precision=HIGHEST, preferred_element_type=F32)
+        own = lax.dot_general(vj[it, :, lanes(c, WIDTH)], gram[...], NT, precision=HIGHEST, preferred_element_type=F32)
         if wait_gram:
             wait(gother, gsem)
         fb[it, zl] = own + lax.dot_general(
-            vj[it, :, lanes(1 - c, WIDTH)], gother[...], nt, precision=HIGHEST, preferred_element_type=F32
+            vj[it, :, lanes(1 - c, WIDTH)], gother[...], NT, precision=HIGHEST, preferred_element_type=F32
         )
         for peer in zmates:
             copy(fb.at[it, zl], fb.at[it, zl], fsem.at[4 * it + zl], peer)
@@ -426,7 +422,7 @@
             pl.when(when)(made.wait_send)
 
 
-def solve(counters, targets, frow, zcol):
+def solve(counters, frow, zcol, right):
     vmem = pl.BlockSpec(memory_space=pltpu.VMEM)
     dma = pltpu.SemaphoreType.DMA
     vector, some = (TARGETS, BLOCK), (TARGETS // 2, BLOCK)
@@ -444,7 +440,6 @@
         in_specs=[vmem] * 4,
         out_specs=(vmem,) * 3,
         scratch_shapes=[
-            pltpu.VMEM(vector, F32),
             pltpu.VMEM((2 * BLOCK, DEPTH + 128), jnp.bfloat16),
             pltpu.VMEM((2 * BLOCK, WIDTH), F32),
         ]
@@ -455,12 +450,13 @@
         ],
         compiler_params=pltpu.CompilerParams(collective_id=1, has_side_effects=True, vmem_limit_bytes=40 << 20),
         name="solve",
-    )(counters.reshape(4 * ROWS, DEPTH), targets, frow, zcol.reshape(4 * ROWS, WIDTH))
+    )(counters.reshape(4 * ROWS, DEPTH), frow, zcol.reshape(4 * ROWS, WIDTH), right)
 
 
 def on_device(counters, frequencies, phases, targets):
     columns = jnp.concatenate([frequencies.T, jnp.broadcast_to(phases.T, (WIDTH, 128))], axis=1)
-    solution, residual, gram = solve(*gather(counters, targets.T, columns, frequencies, phases))
+    samples, _, rows, zcol, right = gather(counters, targets.T, columns, frequencies, phases)
+    solution, residual, gram = solve(samples, rows, zcol, right)
     return solution.T, residual.T, gram
 
 

time: 115 us -> 113 us (0.983)
  Pallas kernels: 110 us -> 108 us
    pallas_call x1, Pallas kernels: 75.9 us -> 72.3 us  [solve(): pl.pallas_call(solve_kernel, out_shape=(jax.ShapeDtypeStruct(vector, F32)...]
    pallas_call x1, Pallas kernels: 33.8 us -> 35.6 us  [gather(): pl.pallas_call(gather_kernel, out_shape=(jax.ShapeDtypeStruct((4, ROWS, D...]
where the time goes in v6:
time: 113 us
  Pallas kernels  108 us (96%)
  local copies, waits for them, and re-layouts  3.34 us (3%)
    pallas_call x1, Pallas kernels, solve(): pl.pallas_call(solve_kernel, out_shape=(jax.ShapeDtypeStruct(vector, F32)...  72.3 us
    pallas_call x1, Pallas kernels, gather(): pl.pallas_call(gather_kernel, out_shape=(jax.ShapeDtypeStruct((4, ROWS, D...  35.6 us
    unnamed x12, local copies, waits for them, and re-layouts  3.21 us

profile of v6, /device:TPU:1, one launch (start us, length us, event | category | flops | bytes accessed | tf_op | source)
XLA Modules:
  0.0 112.9 jit_solution(12960878878964025229)
XLA Ops:
  0.6 0.0 copy-start.3
  0.6 0.0 copy-start
  0.7 0.0 copy-start.2
  0.7 0.0 copy-start.1
  0.7 0.8 reduce
  1.5 0.1 broadcast_in_dim.8
  1.6 1.3 %copy.7 = bf16[512,512]{0,1:T(8,128)(2,1)S(1)} copy(bf16[512,512]{1,0:T(8,128)(2,1)} %fcol.1) | data formatting | bytes 1048576 | tf_op args[1]
  2.9 0.1 pad_maximum_fusion.frq
  3.0 0.0 copy-done.3
  3.0 0.0 copy-done
  3.0 0.0 copy-done.2
  3.0 0.0 copy-done.1
  3.0 35.6 %gather.1 = (bf16[4,1024,512]{2,1,0:T(8,128)(2,1)S(1)}, bf16[4,64,1024]{2,1,0:T(8,128)(2,1)}, bf16[1024,640]{1,0:T(8,128)(2,1)S(1)}, bf16[4,1024,512]{2,1,0:T(8,128)(2,1)S(1)}, f32[64,128]{1,0:T(8,128)S(1)}) custom-call(bf16[1024,512]{1,0:T(8,128)(2,1)S(1)} %copy-done.1, bf16[64,1024]{1,0:T(8,128)(2,1)S(1)} %bitcast.8, ...), custom_call_target="tpu_custom_call" | custom-call | tf_op jit(solution)/shard_map/gather/pallas_call | solution.py:179
  38.6 72.3 %solve.1 = (f32[64,128]{1,0:T(8,128)S(1)}, f32[64,128]{1,0:T(8,128)S(1)}, f32[128,512]{1,0:T(8,128)S(1)}) custom-call(bf16[4096,512]{1,0:T(8,128)(2,1)S(1)} %bitcast.6, bf16[1024,640]{1,0:T(8,128)(2,1)S(1)} %get-tuple-element.11.frow, bf16[4096,512]{1,0:T(8,128)(2,1)S(1)} %bitcast.7, f32[64,128]{1,0:T(8,128)S(1)} %get-tuple-element.13.right), custom_call_target="tpu_custom_call" | custom-call | tf_op jit(solution)/shard_map/solve/pallas_call | solution.py:433
  110.9 0.6 copy.11
  111.6 0.6 copy.12
  112.2 0.7 copy.13
Async XLA Ops:
  0.6 2.3 %copy-start.3 = (bf16[1,512]{1,0:T(2,128)(2,1)S(1)}, bf16[1,512]{1,0:T(2,128)(2,1)}, u32[]{:S(2)}) copy-start(bf16[1,512]{1,0:T(2,128)(2,1)} %phase.1) | copy-start | bytes 3076
  0.6 2.3 %copy-start = (bf16[512,512]{1,0:T(8,128)(2,1)S(1)}, bf16[512,512]{1,0:T(8,128)(2,1)}, u32[]{:S(2)}) copy-start(bf16[512,512]{1,0:T(8,128)(2,1)} %fcol.1) | copy-start | bytes 1572868
  0.7 2.3 %copy-start.2 = (bf16[1024,64]{0,1:T(8,128)(2,1)S(1)}, bf16[1024,64]{0,1:T(8,128)(2,1)}, u32[]{:S(2)}) copy-start(bf16[1024,64]{0,1:T(8,128)(2,1)} %param.7) | copy-start | bytes 393220
  0.7 2.3 %copy-start.1 = (bf16[1024,512]{1,0:T(8,128)(2,1)S(1)}, bf16[1024,512]{1,0:T(8,128)(2,1)}, u32[]{:S(2)}) copy-start(bf16[1024,512]{1,0:T(8,128)(2,1)} %cnt.1) | copy-start | bytes 3145732

commit v7 on v6

--- a/solution.py
+++ b/solution.py
@@ -109,26 +109,25 @@
 
     go(to_right[0])
     go(to_left[1])
-    quarter = pl.ds(pl.multiple_of(BLOCK * x, BLOCK), BLOCK)
     mine = pl.ds(pl.multiple_of(BLOCK * j, BLOCK), BLOCK)
     spread = []
     for i, (dz, core) in enumerate([(1, 0), (1, 1), (-1, 0), (-1, 1), (far, 0), (far, 1)]):
-        spread.append(remote(frq.at[quarter], fr.at[mine], fsend.at[i], frecv.at[2 * (i // 2) + c], along_z(dz, core)))
-    spread.append(remote(frq.at[quarter], fr.at[mine], fsend.at[6], frecv.at[6], sibling))
+        spread.append(remote(frq, fr.at[mine], fsend.at[i], frecv.at[2 * (i // 2) + c], along_z(dz, core)))
+    spread.append(remote(frq, fr.at[mine], fsend.at[6], frecv.at[6], sibling))
     go(spread)
     go(to_right[1])
     go(to_left[0])
     local = [
         pltpu.make_async_copy(cnt, cg.at[0], lsem.at[0]),
         pltpu.make_async_copy(tgt, tg.at[0], lsem.at[1]),
-        pltpu.make_async_copy(frq.at[quarter], fr.at[mine], lsem.at[2]),
+        pltpu.make_async_copy(frq, fr.at[mine], lsem.at[2]),
     ]
     go(local)
     def columns(slot, rows):
         mixed = jnp.dot(cg[slot, rows, :], fcol[...], preferred_element_type=F32)
         zcol[slot, rows, :] = cosine(mixed + phase[...].astype(F32))
         samples = pl.ds(pl.multiple_of(rows.start, STEP), STEP)
-        own = features(frq[quarter, :], cg[slot, rows, :])
+        own = features(frq[...], cg[slot, rows, :])
         rpart[...] += lax.dot_general(tg[slot, :, samples], own, NT, preferred_element_type=F32)
 
     here, there = pl.ds(pl.multiple_of(half, STEP), STEP), pl.ds(pl.multiple_of(STEP - half, STEP), STEP)
@@ -151,20 +150,26 @@
     columns(2, here)
     got(on_right)
     go(across[3, 0])
+
+    def twins(slot):
+        for part in (0, 1):
+            got(twin(6 + 2 * (slot - 1) + part, slot, part))
+
+    twins(1)
+    columns(1, there)
     got(on_left)
     go(across[3, 1])
-    for slot in (1, 2, 3):
-        if slot == 3:
-            columns(3, here)
-        for part in (0, 1):
-            got(twin(6 + 2 * (slot - 1) + part, slot, part))
-        columns(slot, there)
+    twins(2)
+    columns(2, there)
+    columns(3, here)
+    twins(3)
+    columns(3, there)
     for i, (dz, core) in enumerate([(-1, 0), (-1, 1), (1, 0), (1, 1), (-2, 0), (2, 1)]):
         source = along_z(dz, core)
         rows = pl.ds(pl.multiple_of(BLOCK * source[1], BLOCK), BLOCK)
-        remote(frq.at[quarter], fr.at[rows], fsend.at[i], frecv.at[2 * (i // 2) + core], source).wait_recv()
+        remote(frq, fr.at[rows], fsend.at[i], frecv.at[2 * (i // 2) + core], source).wait_recv()
     rows = pl.ds(pl.multiple_of(BLOCK * sibling[1], BLOCK), BLOCK)
-    remote(frq.at[quarter], fr.at[rows], fsend.at[6], frecv.at[6], sibling).wait_recv()
+    remote(frq, fr.at[rows], fsend.at[6], frecv.at[6], sibling).wait_recv()
     local[2].wait()
     sent = to_right[0] + to_right[1] + to_left[0] + to_left[1] + on_right + on_left + spread
     for copies in across.values():
@@ -454,7 +459,10 @@
 
 
 def on_device(counters, frequencies, phases, targets):
-    columns = jnp.concatenate([frequencies.T, jnp.broadcast_to(phases.T, (WIDTH, 128))], axis=1)
+    first = lax.rem(lax.axis_index("samp"), 4) * BLOCK
+    quarter = lax.dynamic_slice_in_dim(frequencies, first, BLOCK, 1).T
+    shift = lax.dynamic_slice_in_dim(phases, first, BLOCK, 1).T
+    columns = jnp.concatenate([quarter, jnp.broadcast_to(shift, (BLOCK, 128))], axis=1)
     samples, _, rows, zcol, right = gather(counters, targets.T, columns, frequencies, phases)
     solution, residual, gram = solve(samples, rows, zcol, right)
     return solution.T, residual.T, gram

time: 113 us -> 118 us (1.044)
  local copies, waits for them, and re-layouts: 3.34 us -> 7.56 us
  Pallas kernels: 108 us -> 110 us
    unnamed x12, local copies, waits for them, and re-layouts: 3.21 us -> 5.89 us
    pallas_call x1, Pallas kernels: 72.3 us -> 74.3 us  [solve(): pl.pallas_call(solve_kernel, out_shape=(jax.ShapeDtypeStruct(vector, F32)...]
where the time goes in v7:
time: 118 us
  Pallas kernels  110 us (93%)
  local copies, waits for them, and re-layouts  7.56 us (6%)
    pallas_call x1, Pallas kernels, solve(): pl.pallas_call(solve_kernel, out_shape=(jax.ShapeDtypeStruct(vector, F32)...  74.3 us
    pallas_call x1, Pallas kernels, gather(): pl.pallas_call(gather_kernel, out_shape=(jax.ShapeDtypeStruct((4, ROWS, D...  35.4 us
    unnamed x12, local copies, waits for them, and re-layouts  5.89 us

profile of v7, /device:TPU:1, one launch (start us, length us, event | category | flops | bytes accessed | tf_op | source)
XLA Modules:
  0.0 117.9 jit_solution(9795125165293436035)
XLA Ops:
  0.6 0.7 dynamic-slice_bitcast_fusion
  1.3 0.1 broadcast_in_dim.8
  1.4 0.9 constant_dynamic-slice_fusion
  2.3 0.1 copy.8
  2.5 0.0 copy-start
  2.5 1.2 %copy-done = bf16[1024,512]{1,0:T(8,128)(2,1)S(1)} copy-done((bf16[1024,512]{1,0:T(8,128)(2,1)S(1)}, bf16[1024,512]{1,0:T(8,128)(2,1)}, u32[]{:S(2)}) %copy-start) | copy-done | bytes 1048600
  3.7 0.0 copy-start.1
  3.7 1.0 copy-done.1
  4.7 0.0 copy-start.2
  4.7 0.9 copy-done.2
  5.6 0.0 copy-start.3
  5.6 0.7 copy-done.3
  6.3 35.4 %gather.1 = (bf16[4,1024,512]{2,1,0:T(8,128)(2,1)S(1)}, bf16[4,64,1024]{2,1,0:T(8,128)(2,1)}, bf16[1024,640]{1,0:T(8,128)(2,1)S(1)}, bf16[4,1024,512]{2,1,0:T(8,128)(2,1)S(1)}, f32[64,128]{1,0:T(8,128)S(1)}) custom-call(bf16[1024,512]{1,0:T(8,128)(2,1)S(1)} %copy-done, bf16[64,1024]{1,0:T(8,128)(2,1)S(1)} %bitcast.10, ...), custom_call_target="tpu_custom_call" | custom-call | tf_op jit(solution)/shard_map/gather/pallas_call | solution.py:184
  41.7 74.3 %solve.1 = (f32[64,128]{1,0:T(8,128)S(1)}, f32[64,128]{1,0:T(8,128)S(1)}, f32[128,512]{1,0:T(8,128)S(1)}) custom-call(bf16[4096,512]{1,0:T(8,128)(2,1)S(1)} %bitcast.8, bf16[1024,640]{1,0:T(8,128)(2,1)S(1)} %get-tuple-element.11.frow, bf16[4096,512]{1,0:T(8,128)(2,1)S(1)} %bitcast.9, f32[64,128]{1,0:T(8,128)S(1)} %get-tuple-element.13.right), custom_call_target="tpu_custom_call" | custom-call | tf_op jit(solution)/shard_map/solve/pallas_call | solution.py:438
  116.0 0.6 copy.12
  116.6 0.6 copy.13
  117.2 0.7 copy.14
  (1 shorter events, 0.0 us)
Async XLA Ops:
  2.5 1.2 %copy-start = (bf16[1024,512]{1,0:T(8,128)(2,1)S(1)}, bf16[1024,512]{1,0:T(8,128)(2,1)}, u32[]{:S(2)}) copy-start(bf16[1024,512]{1,0:T(8,128)(2,1)} %cnt.1) | copy-start | bytes 3145732
  3.7 1.0 copy-start.1
  4.7 0.9 copy-start.2
  5.6 0.7 copy-start.3

commit v8 on v6

--- a/solution.py
+++ b/solution.py
@@ -49,7 +49,7 @@
     pl.semaphore_wait(barrier, len(peers))
 
 
-def gather_kernel(cnt, tgt, frq, fcol, phase, cg, tg, fr, zcol, rpart, ssem, rsem, fsend, frecv, lsem):
+def gather_kernel(cnt, tgt, frq, fcol, phase, cg, fr, zcol, rpart, tg, ssem, rsem, fsend, frecv, lsem):
     s, j = lax.axis_index("samp"), lax.axis_index("feat")
     x, c, zl, zh = lax.rem(s, 4), lax.rem(j, 2), lax.div(j, 2), lax.div(s, 16)
     z = zh * 4 + zl
@@ -151,14 +151,20 @@
     columns(2, here)
     got(on_right)
     go(across[3, 0])
+
+    def twins(slot):
+        for part in (0, 1):
+            got(twin(6 + 2 * (slot - 1) + part, slot, part))
+
+    twins(1)
+    columns(1, there)
     got(on_left)
     go(across[3, 1])
-    for slot in (1, 2, 3):
-        if slot == 3:
-            columns(3, here)
-        for part in (0, 1):
-            got(twin(6 + 2 * (slot - 1) + part, slot, part))
-        columns(slot, there)
+    twins(2)
+    columns(2, there)
+    columns(3, here)
+    twins(3)
+    columns(3, there)
     for i, (dz, core) in enumerate([(-1, 0), (-1, 1), (1, 0), (1, 1), (-2, 0), (2, 1)]):
         source = along_z(dz, core)
         rows = pl.ds(pl.multiple_of(BLOCK * source[1], BLOCK), BLOCK)
@@ -180,14 +186,14 @@
         gather_kernel,
         out_shape=(
             jax.ShapeDtypeStruct((4, ROWS, DEPTH), bf16),
-            jax.ShapeDtypeStruct((4, TARGETS, ROWS), bf16),
             jax.ShapeDtypeStruct((8 * BLOCK, DEPTH + 128), bf16),
             jax.ShapeDtypeStruct((4, ROWS, WIDTH), bf16),
             jax.ShapeDtypeStruct((TARGETS, BLOCK), F32),
         ),
         in_specs=[vmem] * 5,
-        out_specs=(vmem,) * 5,
+        out_specs=(vmem,) * 4,
         scratch_shapes=[
+            pltpu.VMEM((4, TARGETS, ROWS), bf16),
             pltpu.SemaphoreType.DMA((24,)),
             pltpu.SemaphoreType.DMA((24,)),
             pltpu.SemaphoreType.DMA((7,)),
@@ -455,7 +461,7 @@
 
 def on_device(counters, frequencies, phases, targets):
     columns = jnp.concatenate([frequencies.T, jnp.broadcast_to(phases.T, (WIDTH, 128))], axis=1)
-    samples, _, rows, zcol, right = gather(counters, targets.T, columns, frequencies, phases)
+    samples, rows, zcol, right = gather(counters, targets.T, columns, frequencies, phases)
     solution, residual, gram = solve(samples, rows, zcol, right)
     return solution.T, residual.T, gram
 

time: 113 us -> 114 us (level)
    pallas_call x1, Pallas kernels: 72.3 us -> 74.2 us  [solve(): pl.pallas_call(solve_kernel, out_shape=(jax.ShapeDtypeStruct(vector, F32)...]
where the time goes in v8:
time: 114 us
  Pallas kernels  109 us (96%)
  local copies, waits for them, and re-layouts  3.34 us (3%)
    pallas_call x1, Pallas kernels, solve(): pl.pallas_call(solve_kernel, out_shape=(jax.ShapeDtypeStruct(vector, F32)...  74.2 us
    pallas_call x1, Pallas kernels, gather(): pl.pallas_call(gather_kernel, out_shape=(jax.ShapeDtypeStruct((4, ROWS, D...  34.8 us
    unnamed x12, local copies, waits for them, and re-layouts  3.21 us

profile of v8, /device:TPU:1, one launch (start us, length us, event | category | flops | bytes accessed | tf_op | source)
XLA Modules:
  0.0 114.0 jit_solution(10317548542793040982)
XLA Ops:
  0.6 0.0 copy-start.3
  0.6 0.0 copy-start
  0.7 0.0 copy-start.2
  0.7 0.0 copy-start.1
  0.7 0.8 reduce
  1.5 0.1 broadcast_in_dim.8
  1.6 1.3 %copy.7 = bf16[512,512]{0,1:T(8,128)(2,1)S(1)} copy(bf16[512,512]{1,0:T(8,128)(2,1)} %fcol.1) | data formatting | bytes 1048576 | tf_op args[1]
  2.9 0.1 pad_maximum_fusion.frq
  3.0 0.0 copy-done.3
  3.0 0.0 copy-done
  3.0 0.0 copy-done.2
  3.0 0.0 copy-done.1
  3.0 34.8 %gather.1 = (bf16[4,1024,512]{2,1,0:T(8,128)(2,1)S(1)}, bf16[1024,640]{1,0:T(8,128)(2,1)S(1)}, bf16[4,1024,512]{2,1,0:T(8,128)(2,1)S(1)}, f32[64,128]{1,0:T(8,128)S(1)}) custom-call(bf16[1024,512]{1,0:T(8,128)(2,1)S(1)} %copy-done.1, bf16[64,1024]{1,0:T(8,128)(2,1)S(1)} %bitcast.8, bf16[512,640]{1,0:T(8,128)(2,1)S(1)} %pad_maximum_fusion.frq, ...), custom_call_target="tpu_custom_call" | custom-call | tf_op jit(solution)/shard_map/gather/pallas_call | solution.py:185
  37.8 74.2 %solve.1 = (f32[64,128]{1,0:T(8,128)S(1)}, f32[64,128]{1,0:T(8,128)S(1)}, f32[128,512]{1,0:T(8,128)S(1)}) custom-call(bf16[4096,512]{1,0:T(8,128)(2,1)S(1)} %bitcast.6, bf16[1024,640]{1,0:T(8,128)(2,1)S(1)} %get-tuple-element.11.frow, bf16[4096,512]{1,0:T(8,128)(2,1)S(1)} %bitcast.7, f32[64,128]{1,0:T(8,128)S(1)} %get-tuple-element.13.right), custom_call_target="tpu_custom_call" | custom-call | tf_op jit(solution)/shard_map/solve/pallas_call | solution.py:439
  112.0 0.6 copy.11
  112.7 0.6 copy.12
  113.3 0.7 copy.13
Async XLA Ops:
  0.6 2.3 %copy-start.3 = (bf16[1,512]{1,0:T(2,128)(2,1)S(1)}, bf16[1,512]{1,0:T(2,128)(2,1)}, u32[]{:S(2)}) copy-start(bf16[1,512]{1,0:T(2,128)(2,1)} %phase.1) | copy-start | bytes 3076
  0.6 2.3 %copy-start = (bf16[512,512]{1,0:T(8,128)(2,1)S(1)}, bf16[512,512]{1,0:T(8,128)(2,1)}, u32[]{:S(2)}) copy-start(bf16[512,512]{1,0:T(8,128)(2,1)} %fcol.1) | copy-start | bytes 1572868
  0.7 2.3 %copy-start.2 = (bf16[1024,64]{0,1:T(8,128)(2,1)S(1)}, bf16[1024,64]{0,1:T(8,128)(2,1)}, u32[]{:S(2)}) copy-start(bf16[1024,64]{0,1:T(8,128)(2,1)} %param.7) | copy-start | bytes 393220
  0.7 2.3 %copy-start.1 = (bf16[1024,512]{1,0:T(8,128)(2,1)S(1)}, bf16[1024,512]{1,0:T(8,128)(2,1)}, u32[]{:S(2)}) copy-start(bf16[1024,512]{1,0:T(8,128)(2,1)} %cnt.1) | copy-start | bytes 3145732
